TPU v7x, 256 devices: a whole 4x4x8 slice. The times are simulated.
256 devices in a mesh: row: 32 (over z_lo, x, core), col: 8 (over z_hi, y).
Axes of the slice: x: 4, y: 4, z: 8 (z_hi: 2, z_lo: 4; z = z_hi * 4 + z_lo), core: 2. Of those that a mesh axis runs over, the one named last changes fastest.
Arguments:
- positions: float32 [3, 1048576], P(None, ('row', 'col')), may hold values from 0 to 385, as said below
- atom_type: int32 [1048576], P(('row', 'col')), may hold values from 0 to 5
- krylov: float32 [16, 1048576], P(None, ('row', 'col')), may hold values from -6 to 6
- block_order: int32 [1048576], P(('row', 'col')), may hold values from 0 to 4095, as said below
- type_width: float32 [6], replicated, may hold values from 0.5 to 2.5
- type_hard: float32 [6], replicated, may hold values from 1 to 4
- pair_rows: int32 [32, 8, 512], P('row', 'col'), may hold values from 0 to 255, as said below
- pair_cols: int32 [32, 8, 512], P('row', 'col'), may hold values from 0 to 1023, as said below
- pair_count: int32 [32, 8], P('row', 'col'), may hold values from 1 to 512, as said below
Outputs:
- coulomb_response: float32 [16, 1048576], P(None, ('row', 'col'))
Inputs may be any that keep to these rules, and one draw needn't show every extreme that they name: `positions`: global block g is a cell of a grid with coordinates (g // 256, (g // 32) % 8, g % 32); each atom of block g lies in the box of sides 44, 30 and 44 whose lowest corner is the cell's coordinates times 11, 5 and 11. `block_order`: within each device's shard of 4096 atoms, the entries are a permutation of 0 to 4095. `pair_rows`: in slots below pair_count the pairs (i, j) are distinct, have i <= j, and their grid cells differ by at most 2 along the first and third dimensions and at most 4 along the second; for device (r, c), pair_cols // 32 is r, r + 1 or r + 2 there. Other slots hold indices in range that are not used. `pair_cols`: see pair_rows. `pair_count`: some device's list is full.
All inputs are finite; a program needn't handle non-finite values.
Results may differ from a plain program's by a relative error of at most 0.00665.
Values may be sent and summed in bfloat16 or wider, within the bound.
No kernel may reach another device: no remote copies, remote signals or barrier semaphores. Data moves between devices by JAX's collectives and lax.ppermute only.
A program may use at most 128 MiB of HBM per device.

v0:
```python
import functools

import jax
import jax.numpy as jnp
from jax import lax
from jax.experimental import pallas as pl
from jax.experimental.pallas import tpu as pltpu
from jax.sharding import PartitionSpec as P

BLK = 128
VECS = 16
NTYPES = 6
BLOCKS = 32
HALF = 4 * BLOCKS
COLS = 3 * BLOCKS
ROWS = VECS + 8
DEPTH = 80
UNROLL = 8
SLOTS = 512
SLOT_SPAN = SLOTS + UNROLL
CELL = (11.0, 5.0, 11.0)
BOX = (44.0, 30.0, 44.0)
SOFTENING = 0.5

ERF_COEFFS = (
    1.1283815681128107,
    -7.621837438329706e-05,
    0.10341113638200404,
    -0.002217632183960096,
    0.003526363187890101,
    -0.0031284691084128495,
    0.0005233424709803657,
)

PAIR_COST = pl.CostEstimate(flops=16_000_000_000, transcendentals=0, bytes_accessed=8_000_000)

VMEM = pl.BlockSpec(memory_space=pltpu.VMEM)
SMEM = pl.BlockSpec(memory_space=pltpu.SMEM)
Y_GROUPS = [[0, 1, 2, 3], [4, 5, 6, 7]]
F32 = jnp.float32
BF16 = jnp.bfloat16


def sublane():
    return lax.broadcasted_iota(jnp.int32, (8, BLK), 0)


def split3(value):
    high = value.astype(BF16).astype(F32)
    rest = value - high
    middle = rest.astype(BF16).astype(F32)
    return high, middle, rest - middle


def lane_gather(source, index):
    return jnp.take_along_axis(source, index, axis=1, mode="promise_in_bounds")


def prep_kernel(place, positions, atom_type, krylov, order, packed, geometry):
    geometry[...] = jnp.zeros_like(geometry)
    geometry[0:3, :] = positions[...]
    geometry[3:4, :] = atom_type[...].astype(F32)
    level = sublane()
    corner_x = CELL[0] * place[0].astype(F32) + BOX[0] / 2
    corner_y = CELL[1] * place[1].astype(F32) + BOX[1] / 2

    def one_block(block, carry):
        wanted = jnp.broadcast_to(order[pl.ds(block, 1), :], (8, BLK))
        chunk = wanted >> 7
        lane = wanted & 127
        top = jnp.zeros((8, BLK), F32)
        low = jnp.zeros((8, BLK), F32)
        geo = jnp.zeros((8, BLK), F32)
        for s in range(BLOCKS):
            here = chunk == s
            span = slice(s * BLK, (s + 1) * BLK)
            top = jnp.where(here, lane_gather(krylov[0:8, span], lane), top)
            low = jnp.where(here, lane_gather(krylov[8:16, span], lane), low)
            geo = jnp.where(here, lane_gather(geometry[:, span], lane), geo)
        corner_z = CELL[2] * block.astype(F32) + BOX[2] / 2
        corner = jnp.where(
            level == 0, corner_x, jnp.where(level == 1, corner_y, jnp.where(level == 2, corner_z, 0.0))
        )
        local = geo - corner
        coarse = jnp.floor(local * 4.0 + 0.5) * 0.25
        fine = jnp.where(level < 3, local - coarse, local)
        coded = jnp.where(level < 3, coarse, pltpu.roll(fine, 3, 0))
        packed[block, 0:VECS, :] = jnp.concatenate([top, low], axis=0).astype(BF16)
        packed[block, VECS:ROWS, :] = coded.astype(BF16)
        return carry

    lax.fori_loop(0, BLOCKS, one_block, 0)


def side_kernel(place, rows, cols, count, order, inverse, codes, counts):
    row_index = place[0]
    col_index = place[1]
    own_half = col_index >> 2

    live = count[0]

    def some_slots(turn, seen):
        first, second = seen
        for extra in range(4):
            slot = turn * 4 + extra
            row = rows[slot]
            col = cols[slot] - row_index * BLOCKS
            same = (row >> 7) == own_half
            diagonal = jnp.logical_and(col < BLOCKS, row == col_index * BLOCKS + col)
            code = (
                (row & 127)
                | (col << 7)
                | ((col_index - (row >> 5) + 4) << 14)
                | (((col & 31) - (row & 31) + 2) << 18)
                | (diagonal.astype(jnp.int32) << 21)
            )
            used = slot < live
            target = jnp.where(same, first, SLOT_SPAN + second)
            codes[jnp.where(used, target, 2 * SLOT_SPAN)] = code
            one = jnp.logical_and(used, same).astype(jnp.int32)
            second = second + used.astype(jnp.int32) - one
            first = first + one
        return first, second

    first, second = lax.fori_loop(0, (live + 3) // 4, some_slots, (jnp.int32(0), jnp.int32(0)))
    spare = (4 << 14) | (2 << 18) | (1 << 21) | (1 << 22)
    for extra in range(UNROLL):
        codes[first + extra] = spare
        codes[SLOT_SPAN + second + extra] = spare
    counts[0] = first
    counts[1] = second

    level_h = lax.broadcasted_iota(jnp.int32, (BLOCKS, BLK), 0)
    level_l = lax.broadcasted_iota(jnp.int32, (BLK, BLK), 0)
    lanes = lax.broadcasted_iota(jnp.int32, (BLOCKS, BLK), 1).astype(F32)
    total = jnp.zeros((2 * BLOCKS, BLK), F32)
    for block in range(BLOCKS):
        wanted = order[block : block + 1, :]
        in_high = (level_h == jnp.broadcast_to(wanted >> 7, (BLOCKS, BLK))).astype(F32)
        in_low = (level_l == jnp.broadcast_to(wanted & 127, (BLK, BLK))).astype(F32).astype(BF16)
        left = jnp.concatenate([in_high * float(block), in_high * lanes], axis=0).astype(BF16)
        total = total + lax.dot_general(
            left, in_low, (((1,), (1,)), ((), ())), preferred_element_type=F32
        )
    inverse[...] = (total[0:BLOCKS] * float(BLK) + total[BLOCKS:]).astype(jnp.int32)


def feature_kernel(type_width, own, after, second, features, vectors):
    level = sublane()
    squares = jnp.zeros((8, BLK), F32)
    for t in range(NTYPES):
        squares = jnp.where(level == t, type_width[t] * type_width[t], squares)
    low3 = level < 3
    low6 = level < 6
    last = level == 7
    zero = jnp.zeros((8, BLK), F32)
    ones = jnp.where(low6, 1.0, 0.0)
    twos = jnp.where(jnp.logical_and(low6, level >= 3), 2.0, 0.0)

    for part, source in enumerate((own, after, second)):

        def one_block(block, part=part, source=source):
            vectors[part * BLOCKS + block] = source[block, 0:VECS, :]
            coded = source[block, VECS:ROWS, :].astype(F32)
            near = coded + pltpu.roll(coded, 5, 0)
            square = near * near
            weight = square[0:1] + square[1:2] + square[2:3] + SOFTENING * SOFTENING
            weight_h, weight_m, weight_l = split3(weight)
            coarse = jnp.where(low3, coded, pltpu.roll(coded, 3, 0)) * -2.0
            fine = jnp.where(low3, pltpu.roll(coded, 5, 0), coded) * -2.0
            own_type = jnp.broadcast_to(coded[6:7], (8, BLK))
            own_square = jnp.zeros((8, BLK), F32)
            for t in range(NTYPES):
                own_square = jnp.where(own_type == float(t), type_width[t] * type_width[t], own_square)
            scale = lax.rsqrt(own_square + squares)
            scale_h, scale_m, scale_l = split3(jnp.where(low6, scale, 0.0))
            wide = lambda v: jnp.broadcast_to(v, (8, BLK))
            stacked = jnp.concatenate(
                [
                    jnp.where(low6, coarse, jnp.where(last, wide(weight_h), 0.0)),
                    jnp.where(low6, fine, jnp.where(last, wide(weight_m), 0.0)),
                    jnp.where(last, wide(weight_l), ones),
                    ones,
                    twos,
                    twos,
                    scale_h,
                    scale_m,
                    scale_l,
                ]
                + [zero] * 7,
                axis=0,
            )
            features[part * BLOCKS + block] = stacked.T.astype(BF16)

        def some_blocks(turn, carry, one_block=one_block):
            for extra in range(4):
                one_block(turn * 4 + extra)
            return carry

        lax.fori_loop(0, BLOCKS // 4, some_blocks, 0)


def pair_operand(code, row_data, steps):
    coded = row_data[code & 127, VECS:ROWS, :].astype(F32)
    col = (code >> 7) & 127
    shift = steps[col >> 5] + steps[3 + ((code >> 14) & 15)] + steps[12 + ((code >> 18) & 7)]
    near = coded - shift
    square = near * near
    cross = near * pltpu.roll(near, 3, 0)
    square_h = square.astype(BF16).astype(F32)
    cross_h = cross.astype(BF16).astype(F32)
    hot = (sublane().astype(F32) == jnp.broadcast_to(coded[6:7], (8, BLK))).astype(F32)
    zero = jnp.zeros((8, BLK), F32)
    left = jnp.concatenate(
        [near, near, square_h, square - square_h, cross_h, cross - cross_h, zero, zero, zero, zero],
        axis=0,
    ).astype(BF16)
    right = jnp.concatenate([zero] * 6 + [hot, hot, hot, zero], axis=0).astype(BF16)
    return jnp.concatenate([left, right], axis=1)


def tile_values(distance2, scale):
    inverse = lax.rsqrt(distance2)
    z = distance2 * inverse * scale
    poly = ERF_COEFFS[-1]
    for coefficient in ERF_COEFFS[-2::-1]:
        poly = poly * z + coefficient
    return (jnp.tanh(poly * z) * inverse).astype(BF16)


def pair_loop(phase, counts, codes, row_data, vectors, features, steps, row_acc, col_acc, waiting, tiles):
    base = phase * SLOT_SPAN
    batches = (counts[phase] + UNROLL - 1) // UNROLL

    def one_turn(turn, carry):
        adding = base + jnp.maximum(turn - 2, 0) * UNROLL
        opening = base + jnp.maximum(jnp.minimum(turn, batches - 1), 0) * UNROLL
        sums = []
        for first in range(0, UNROLL, 2):
            done = [codes[adding + first + k] for k in range(2)]
            both = [tiles[first + k] for k in range(2)]
            forward = jnp.dot(
                jnp.concatenate([vectors[(code >> 7) & 127] for code in done], axis=0),
                jnp.concatenate(both, axis=1),
                preferred_element_type=F32,
            )
            backward = lax.dot_general(
                jnp.concatenate([row_data[code & 127, 0:VECS, :] for code in done], axis=0),
                jnp.concatenate(both, axis=0),
                (((1,), (1,)), ((), ())),
                preferred_element_type=F32,
            )
            for k, code in enumerate(done):
                to_row = jnp.where(jnp.logical_or(turn < 2, ((code >> 22) & 1) == 1), HALF, code & 127)
                to_col = jnp.where(
                    jnp.logical_or(turn < 2, ((code >> 21) & 1) == 1), COLS, (code >> 7) & 127
                )
                own = (slice(k * VECS, (k + 1) * VECS), slice(k * BLK, (k + 1) * BLK))
                sums.append((to_row, forward[own], to_col, backward[own]))
            for k in range(2):
                slot = first + k
                tiles[slot] = tile_values(waiting[slot, :, 0:BLK], waiting[slot, :, BLK:])
                code = codes[opening + slot]
                waiting[slot] = jnp.dot(
                    features[(code >> 7) & 127][:, 0:DEPTH],
                    pair_operand(code, row_data, steps),
                    preferred_element_type=F32,
                )
        for to_row, forward, to_col, backward in sums:
            row_acc[to_row] += forward
            col_acc[to_col] += backward
        return carry

    lax.fori_loop(0, batches + 2, one_turn, 0)


def near_far_kernel(phase, *refs):
    place, counts, codes = refs[0:3]
    pieces = refs[3:7]
    vectors, features, steps = refs[7:10]
    col_in = refs[10:11] if phase == 1 else ()
    outs = refs[10 + len(col_in) : -5]
    row_data, row_acc, col_acc, waiting, tiles = refs[-5:]
    position = place[1] & 3
    for k, piece in enumerate(pieces):
        start = pl.multiple_of(((position - k) & 3) * BLOCKS, BLOCKS)
        row_data[pl.ds(start, BLOCKS)] = piece[...]
    row_acc[...] = jnp.zeros_like(row_acc)
    if phase == 0:
        col_acc[...] = jnp.zeros_like(col_acc)
    else:
        col_acc[0:COLS] = col_in[0][...]
    pair_loop(phase, counts, codes, row_data, vectors, features, steps, row_acc, col_acc, waiting, tiles)
    for k in range(4):
        start = pl.multiple_of(((position + k) & 3) * BLOCKS, BLOCKS)
        outs[k][...] = row_acc[pl.ds(start, BLOCKS)].astype(outs[k].dtype)
    if phase == 0:
        outs[4][...] = col_acc[0:COLS]
    else:
        for step in range(3):
            outs[4 + step][...] = col_acc[step * BLOCKS : (step + 1) * BLOCKS].astype(outs[4 + step].dtype)


def sum_kernel(*refs):
    total = refs[0][...].astype(F32)
    for ref in refs[1:-1]:
        total = total + ref[...].astype(F32)
    refs[-1][...] = total.astype(refs[-1].dtype)


def final_kernel(type_hard, *refs):
    atom_type, krylov, inverse, out, blocked = refs[-5:]
    parts = refs[:-5]

    def add_up(block, carry):
        total = parts[0][block]
        for part in parts[1:]:
            total = total + part[block].astype(F32)
        blocked[block] = total
        return carry

    lax.fori_loop(0, BLOCKS, add_up, 0)
    for chunk in range(BLOCKS):
        wanted = jnp.broadcast_to(inverse[chunk : chunk + 1, :], (8, BLK))
        source = wanted >> 7
        lane = wanted & 127
        span = slice(chunk * BLK, (chunk + 1) * BLK)
        kind = jnp.broadcast_to(atom_type[:, span], (8, BLK))
        hard = jnp.zeros((8, BLK), F32)
        for t in range(NTYPES):
            hard = jnp.where(kind == t, type_hard[t], hard)

        def pick(block, carry, source=source, lane=lane):
            top, low = carry
            here = source == block
            top = jnp.where(here, lane_gather(blocked[block, 0:8, :], lane), top)
            low = jnp.where(here, lane_gather(blocked[block, 8:16, :], lane), low)
            return top, low

        start = (hard * 0.0, hard * 0.0)
        top, low = lax.fori_loop(0, BLOCKS, pick, start, unroll=True)
        out[0:8, span] = top + hard * krylov[0:8, span]
        out[8:16, span] = low + hard * krylov[8:16, span]


def shape(dims, dtype):
    return jax.ShapeDtypeStruct(dims, dtype)


def call(kernel, out_shape, in_specs, out_specs, name, scratch=(), vmem=48, cost=None):
    return pl.pallas_call(
        kernel,
        out_shape=out_shape,
        in_specs=in_specs,
        out_specs=out_specs,
        scratch_shapes=list(scratch),
        compiler_params=pltpu.CompilerParams(vmem_limit_bytes=vmem << 20),
        cost_estimate=cost,
        name=name,
    )


def step_tables():
    level = lax.broadcasted_iota(jnp.int32, (17, 8, BLK), 1)
    which = lax.broadcasted_iota(jnp.int32, (17, 8, BLK), 0)
    along_x = jnp.where(level == 0, CELL[0] * which.astype(F32), jnp.where(level == 7, -1.0, 0.0))
    along_y = jnp.where(level == 1, CELL[1] * (which - 7).astype(F32), 0.0)
    along_z = jnp.where(level == 2, CELL[2] * (which - 14).astype(F32), 0.0)
    return jnp.where(which < 3, along_x, jnp.where(which < 12, along_y, along_z))


def passed_down(value, steps):
    count = lax.axis_size("row")
    return lax.ppermute(value, "row", [(s, s - steps) for s in range(steps, count)])


def passed_up(value, steps):
    count = lax.axis_size("row")
    return lax.ppermute(value, "row", [(s, s + steps) for s in range(count - steps)])


def across(value):
    return lax.ppermute(value, "col", [(c, c ^ 4) for c in range(8)])


def around(value, steps):
    return lax.ppermute(value, "col", [(c, (c & 4) + (c + steps) % 4) for c in range(8)])


def on_device(
    positions, atom_type, krylov, block_order, type_width, type_hard, pair_rows, pair_cols, pair_count
):
    place = jnp.stack([lax.axis_index("row"), lax.axis_index("col")]).astype(jnp.int32)
    order = block_order.reshape(BLOCKS, BLK)
    kinds = atom_type.reshape(1, -1)

    packed = call(
        prep_kernel,
        shape((BLOCKS, ROWS, BLK), BF16),
        [SMEM, VMEM, VMEM, VMEM, VMEM],
        VMEM,
        "prep",
        scratch=[pltpu.VMEM((8, BLOCKS * BLK), F32)],
    )(place, positions, kinds, krylov, order)

    other = across(packed)
    near_rows = [packed] + [around(packed, k) for k in (1, 2, 3)]
    after = passed_down(packed, 1)
    second = passed_down(packed, 2)
    far_rows = [other] + [around(other, k) for k in (1, 2, 3)]

    inverse, codes, counts = call(
        side_kernel,
        (
            shape((BLOCKS, BLK), jnp.int32),
            shape((2 * SLOT_SPAN + 1,), jnp.int32),
            shape((2,), jnp.int32),
        ),
        [SMEM, SMEM, SMEM, SMEM, VMEM],
        (VMEM, SMEM, SMEM),
        "side",
    )(place, pair_rows.reshape(-1), pair_cols.reshape(-1), pair_count.reshape(-1), order)

    features, vectors = call(
        feature_kernel,
        (shape((COLS, BLK, BLK), BF16), shape((COLS, VECS, BLK), BF16)),
        [SMEM, VMEM, VMEM, VMEM],
        (VMEM, VMEM),
        "features",
    )(type_width, packed, after, second)

    steps = step_tables()
    scratch = [
        pltpu.VMEM((HALF, ROWS, BLK), BF16),
        pltpu.VMEM((HALF + 1, VECS, BLK), F32),
        pltpu.VMEM((COLS + 1, VECS, BLK), F32),
        pltpu.VMEM((UNROLL, BLK, 2 * BLK), F32),
        pltpu.VMEM((UNROLL, BLK, BLK), BF16),
    ]
    block_set = (BLOCKS, VECS, BLK)
    *near_sums, col_sums = call(
        functools.partial(near_far_kernel, 0),
        [shape(block_set, F32)] + [shape(block_set, BF16)] * 3 + [shape((COLS, VECS, BLK), F32)],
        [SMEM] * 3 + [VMEM] * 7,
        [VMEM] * 5,
        "pairs_near",
        scratch=scratch,
        cost=PAIR_COST,
    )(place, counts, codes, *near_rows, vectors, features, steps)
    near_parts = [near_sums[0]] + [around(near_sums[k], k) for k in (1, 2, 3)]

    *far_sums, own_sum, after_sum, last_sum = call(
        functools.partial(near_far_kernel, 1),
        [shape(block_set, BF16)] * 4 + [shape(block_set, F32)] + [shape(block_set, BF16)] * 2,
        [SMEM] * 3 + [VMEM] * 8,
        [VMEM] * 7,
        "pairs_far",
        scratch=scratch,
        cost=PAIR_COST,
    )(place, counts, codes, *far_rows, vectors, features, steps, col_sums)

    far_parts = [far_sums[0]] + [around(far_sums[k], k) for k in (1, 2, 3)]
    from_prior = passed_up(after_sum, 1)
    from_second = passed_up(last_sum, 2)
    far_sum = call(
        sum_kernel, shape((BLOCKS, VECS, BLK), BF16), [VMEM] * 4, VMEM, "far_sum"
    )(*far_parts)
    from_far = across(far_sum)

    parts = [own_sum, from_prior, from_second, *near_parts, from_far]
    return call(
        final_kernel,
        shape(krylov.shape, F32),
        [SMEM] + [VMEM] * (len(parts) + 3),
        VMEM,
        "final",
        scratch=[pltpu.VMEM((BLOCKS, VECS, BLK), F32)],
    )(type_hard, *parts, kinds, krylov, inverse)


def solution(mesh):
    placed = (
        P(None, ("row", "col")),
        P(("row", "col")),
        P(None, ("row", "col")),
        P(("row", "col")),
        P(),
        P(),
        P("row", "col", None),
        P("row", "col", None),
        P("row", "col"),
    )
    return jax.shard_map(
        on_device, mesh=mesh, in_specs=placed, out_specs=P(None, ("row", "col")), check_vma=False
    )
```

profile of v0, /device:TPU:6, one launch (start us, length us, event | category | flops | bytes accessed | tf_op | source)
XLA Modules:
  0.0 116.4 jit_solution(2602028181661311302)
XLA Ops:
  0.1 0.9 copy-done
  1.0 0.7 copy-done.2
  1.7 0.8 copy-done.4
  2.6 0.7 copy-done.5
  3.3 5.2 %prep.1.own.refs_3_ = bf16[32,24,128]{2,1,0:T(8,128)(2,1)S(1)} custom-call(s32[2]{0:T(128)S(1)} %pad_add_fusion.place.refs_0_, f32[3,4096]{1,0:T(4,128)S(1)} %copy-done.4, s32[1,4096]{1,0:T(1,128)S(1)} %bitcast.8, f32[16,4096]{1,0:T(8,128)S(1)} %copy-done, s32[32,128]{1,0:T(8,128)S(1)} %bitcast.10), custom_call_target="tpu_custom_call" | custom-call | tf_op jit(solution)/shard_map/prep/pallas_call | solution.py:397
  8.5 3.1 %collective-permute-start.8 = (bf16[32,24,128]{2,1,0:T(8,128)(2,1)S(1)}, bf16[32,24,128]{2,1,0:T(8,128)(2,1)S(1)}, u32[]{:S(2)}, u32[]{:S(2)}) collective-permute-start(bf16[32,24,128]{2,1,0:T(8,128)(2,1)S(1)} %prep.1.own.refs_3_), channel_id=1, source_target_pairs={{0,3},{1,0},{2,1},{3,2},{4,7},{5,4},{6,5},{7,6},{8,11},{9,8},{10,9... | collective-permute-start | bytes 589832 | tf_op jit(solution)/shard_map/ppermute | solution.py:387
  11.6 0.6 collective-permute-start.7
  12.2 1.0 collective-permute-start.6
  13.2 2.7 %collective-permute-start.5 = (bf16[32,24,128]{2,1,0:T(8,128)(2,1)S(1)}, bf16[32,24,128]{2,1,0:T(8,128)(2,1)S(1)}, u32[]{:S(2)}, u32[]{:S(2)}) collective-permute-start(bf16[32,24,128]{2,1,0:T(8,128)(2,1)S(1)} %prep.1.own.refs_3_), channel_id=1, source_target_pairs={{16,0},{24,8},{32,16},{40,24},{48,32},{56,40},{64,48},{72,56},{80,... | collective-permute-start | bytes 589832 | tf_op jit(solution)/shard_map/ppermute | solution.py:374
  15.9 1.9 %collective-permute-start.4 = (bf16[32,24,128]{2,1,0:T(8,128)(2,1)S(1)}, bf16[32,24,128]{2,1,0:T(8,128)(2,1)S(1)}, u32[]{:S(2)}, u32[]{:S(2)}) collective-permute-start(bf16[32,24,128]{2,1,0:T(8,128)(2,1)S(1)} %prep.1.own.refs_3_), channel_id=1, source_target_pairs={{8,0},{16,8},{24,16},{32,24},{40,32},{48,40},{56,48},{64,56},{72,6... | collective-permute-start | bytes 589832 | tf_op jit(solution)/shard_map/ppermute | solution.py:374
  18.6 0.7 copy-done.6
  19.3 0.7 copy-done.7
  20.0 0.7 copy-done.8
  20.7 6.3 %side.1 = (s32[32,128]{1,0:T(8,128)S(1)}, s32[1041]{0:T(1024)S(1)}, s32[2]{0:T(128)S(1)}) custom-call(s32[2]{0:T(128)S(1)} %pad_add_fusion.place.refs_0_, s32[512]{0:T(512)S(1)} %bitcast.12, s32[512]{0:T(512)S(1)} %bitcast.13, s32[1]{0:T(128)} %bitcast.7.count, s32[32,128]{1,0:T(8,128)S(1)} %bitcast.11), custom_call_target="tpu_custom_call" | custom-call | tf_op jit(solution)/shard_map/side/pallas_call | solution.py:412
  27.0 5.2 %collective-permute-start = (bf16[32,24,128]{2,1,0:T(8,128)(2,1)S(1)}, bf16[32,24,128]{2,1,0:T(8,128)(2,1)S(1)}, u32[]{:S(2)}, u32[]{:S(2)}) collective-permute-start(bf16[32,24,128]{2,1,0:T(8,128)(2,1)S(1)} %prep.1.own.refs_3_), channel_id=1, source_target_pairs={{0,4},{1,5},{2,6},{3,7},{4,0},{5,1},{6,2},{7,3},{8,12},{9,13},{10,... | collective-permute-start | bytes 589832 | tf_op jit(solution)/shard_map/ppermute | solution.py:383
  32.3 5.4 %collective-permute-done.refs_3_ = bf16[32,24,128]{2,1,0:T(8,128)(2,1)S(1)} collective-permute-done((bf16[32,24,128]{2,1,0:T(8,128)(2,1)S(1)}, bf16[32,24,128]{2,1,0:T(8,128)(2,1)S(1)}, u32[]{:S(2)}, u32[]{:S(2)}) %collective-permute-start) | collective-permute-done | bytes 196640 | tf_op jit(solution)/shard_map/ppermute | solution.py:383
  37.7 0.3 collective-permute-start.3
  38.0 7.3 %collective-permute-start.2 = (bf16[32,24,128]{2,1,0:T(8,128)(2,1)S(1)}, bf16[32,24,128]{2,1,0:T(8,128)(2,1)S(1)}, u32[]{:S(2)}, u32[]{:S(2)}) collective-permute-start(bf16[32,24,128]{2,1,0:T(8,128)(2,1)S(1)} %collective-permute-done.refs_3_), channel_id=1, source_target_pairs={{0,2},{1,3},{2,0},{3,1},{4,6},{5,7},{6,4},{7,5},{8,10},{9,11},{10,... | collective-permute-start | bytes 589832 | tf_op jit(solution)/shard_map/ppermute | solution.py:387
  45.3 0.7 copy-done.9
  46.0 3.6 %features.1 = (bf16[96,128,128]{2,1,0:T(8,128)(2,1)S(1)}, bf16[96,16,128]{2,1,0:T(8,128)(2,1)S(1)}) custom-call(f32[6]{0:T(128)S(1)} %copy-done.9, bf16[32,24,128]{2,1,0:T(8,128)(2,1)S(1)} %prep.1.own.refs_3_, bf16[32,24,128]{2,1,0:T(8,128)(2,1)S(1)} %collective-permute-done.4.after, bf16[32,24,128]{2,1,0:T(8,128)(2,1)S(1)} %collective-permute-done.5.second), custom_call_target="tpu_custom_call" | custom-call | tf_op jit(solution)/shard_map/features/pallas_call | solution.py:424
  49.7 18.9 %pairs_near.1 = (f32[32,16,128]{2,1,0:T(8,128)S(1)}, bf16[32,16,128]{2,1,0:T(8,128)(2,1)S(1)}, bf16[32,16,128]{2,1,0:T(8,128)(2,1)S(1)}, bf16[32,16,128]{2,1,0:T(8,128)(2,1)S(1)}, f32[96,16,128]{2,1,0:T(8,128)S(1)}) custom-call(s32[2]{0:T(128)S(1)} %pad_add_fusion.place.refs_0_, s32[2]{0:T(128)S(1)} %get-tuple-element.22.refs_1_, ...), custom_call_target="tpu_custom_call" | custom-call | flops 16000000000 | bytes 8000000 | tf_op jit(solution)/shard_map/pairs_near/pallas_call | solution.py:441
  68.7 7.8 %pairs_far.1 = (bf16[32,16,128]{2,1,0:T(8,128)(2,1)S(1)}, bf16[32,16,128]{2,1,0:T(8,128)(2,1)S(1)}, bf16[32,16,128]{2,1,0:T(8,128)(2,1)S(1)}, bf16[32,16,128]{2,...) custom-call(s32[2]{0:T(128)S(1)} %pad_add_fusion.place.refs_0_, ...), custom_call_target="tpu_custom_call" | custom-call | flops 16000000000 | bytes 8000000 | tf_op jit(solution)/shard_map/pairs_far/pallas_call | solution.py:452
  76.5 5.6 %collective-permute-start.14 = (bf16[32,16,128]{2,1,0:T(8,128)(2,1)S(1)}, bf16[32,16,128]{2,1,0:T(8,128)(2,1)S(1)}, u32[]{:S(2)}, u32[]{:S(2)}) collective-permute-start(bf16[32,16,128]{2,1,0:T(8,128)(2,1)S(1)} %get-tuple-element.35), channel_id=1, source_target_pairs={{0,1},{1,2},{2,3},{3,0},{4,5},{5,6},{6,7},{7,4},{8,9},{9,10},{10,1... | collective-permute-start | bytes 393224 | tf_op jit(solution)/shard_map/ppermute | solution.py:387
  82.1 2.8 %collective-permute-start.16 = (bf16[32,16,128]{2,1,0:T(8,128)(2,1)S(1)}, bf16[32,16,128]{2,1,0:T(8,128)(2,1)S(1)}, u32[]{:S(2)}, u32[]{:S(2)}) collective-permute-start(bf16[32,16,128]{2,1,0:T(8,128)(2,1)S(1)} %get-tuple-element.37), channel_id=1, source_target_pairs={{0,3},{1,0},{2,1},{3,2},{4,7},{5,4},{6,5},{7,6},{8,11},{9,8},{10,9... | collective-permute-start | bytes 393224 | tf_op jit(solution)/shard_map/ppermute | solution.py:387
  84.9 2.8 %collective-permute-start.12 = (bf16[32,16,128]{2,1,0:T(8,128)(2,1)S(1)}, bf16[32,16,128]{2,1,0:T(8,128)(2,1)S(1)}, u32[]{:S(2)}, u32[]{:S(2)}) collective-permute-start(bf16[32,16,128]{2,1,0:T(8,128)(2,1)S(1)} %get-tuple-element.32), channel_id=1, source_target_pairs={{0,2},{1,3},{2,0},{3,1},{4,6},{5,7},{6,4},{7,5},{8,10},{9,11},{10,... | collective-permute-start | bytes 393224 | tf_op jit(solution)/shard_map/ppermute | solution.py:387
  87.7 0.6 collective-permute-start.13
  88.3 1.7 %collective-permute-done.15.refs_2_ = bf16[32,16,128]{2,1,0:T(8,128)(2,1)S(1)} collective-permute-done((bf16[32,16,128]{2,1,0:T(8,128)(2,1)S(1)}, bf16[32,16,128]{2,1,0:T(8,128)(2,1)S(1)}, u32[]{:S(2)}, u32[]{:S(2)}) %collective-permute-start.15) | collective-permute-done | bytes 131104 | tf_op jit(solution)/shard_map/ppermute | solution.py:387
  90.0 3.5 %collective-permute-start.9 = (bf16[32,16,128]{2,1,0:T(8,128)(2,1)S(1)}, bf16[32,16,128]{2,1,0:T(8,128)(2,1)S(1)}, u32[]{:S(2)}, u32[]{:S(2)}) collective-permute-start(bf16[32,16,128]{2,1,0:T(8,128)(2,1)S(1)} %get-tuple-element.28), channel_id=1, source_target_pairs={{0,8},{8,16},{16,24},{24,32},{32,40},{40,48},{48,56},{56,64},{64,7... | collective-permute-start | bytes 393224 | tf_op jit(solution)/shard_map/ppermute | solution.py:379
  93.5 8.8 %collective-permute-start.10 = (bf16[32,16,128]{2,1,0:T(8,128)(2,1)S(1)}, bf16[32,16,128]{2,1,0:T(8,128)(2,1)S(1)}, u32[]{:S(2)}, u32[]{:S(2)}) collective-permute-start(bf16[32,16,128]{2,1,0:T(8,128)(2,1)S(1)} %get-tuple-element.29), channel_id=1, source_target_pairs={{0,16},{8,24},{16,32},{24,40},{32,48},{40,56},{48,64},{56,72},{64,... | collective-permute-start | bytes 393224 | tf_op jit(solution)/shard_map/ppermute | solution.py:379
  102.6 3.3 %collective-permute-done.10.refs_2_ = bf16[32,16,128]{2,1,0:T(8,128)(2,1)S(1)} collective-permute-done((bf16[32,16,128]{2,1,0:T(8,128)(2,1)S(1)}, bf16[32,16,128]{2,1,0:T(8,128)(2,1)S(1)}, u32[]{:S(2)}, u32[]{:S(2)}) %collective-permute-start.10) | collective-permute-done | bytes 131104 | tf_op jit(solution)/shard_map/ppermute | solution.py:379
  105.9 6.5 %collective-permute-done.17.refs_7_ = bf16[32,16,128]{2,1,0:T(8,128)(2,1)S(1)} collective-permute-done((bf16[32,16,128]{2,1,0:T(8,128)(2,1)S(1)}, bf16[32,16,128]{2,1,0:T(8,128)(2,1)S(1)}, u32[]{:S(2)}, u32[]{:S(2)}) %collective-permute-start.17) | collective-permute-done | bytes 131104 | tf_op jit(solution)/shard_map/ppermute | solution.py:383
  112.4 3.9 %final.1 = f32[16,4096]{1,0:T(8,128)} custom-call(f32[6]{0:T(128)S(1)} %copy-done.10, f32[32,16,128]{2,1,0:T(8,128)S(1)} %get-tuple-element.27.refs_0_, bf16[32,16,128]{2,1,0:T(8,128)(2,1)S(1)} %collective-permute-done.9.refs_1_, bf16[32,16,128]{2,1,0:T(8,128)(2,1)S(1)} %collective-permute-done.10.refs_2_, f32[32,16,128]{2,1,0:T(8,128)S(1)} %get-tuple-element.30.refs_3_, ...), custom_call_target="tpu_custom_call" | custom-call | tf_op jit(solution)/shard_map/final/pallas_call | solution.py:471
  (43 shorter events, 0.6 us)
Async XLA Ops:
  0.1 0.9 copy-start
  1.0 0.7 copy-start.2
  1.7 0.8 copy-start.4
  2.6 0.7 copy-start.5
  8.5 41.0 %collective-permute-start.8 = (bf16[32,24,128]{2,1,0:T(8,128)(2,1)S(1)}, bf16[32,24,128]{2,1,0:T(8,128)(2,1)S(1)}, u32[]{:S(2)}, u32[]{:S(2)}) collective-permute-start(bf16[32,24,128]{2,1,0:T(8,128)(2,1)S(1)} %prep.1.own.refs_3_), channel_id=1, source_target_pairs={{0,3},{1,0},{2,1},{3,2},{4,7},{5,4},{6,5},{7,6},{8,11},{9,8},{10,9... | collective-permute-start | bytes 589832 | tf_op jit(solution)/shard_map/ppermute | solution.py:387
  11.6 38.0 %collective-permute-start.7 = (bf16[32,24,128]{2,1,0:T(8,128)(2,1)S(1)}, bf16[32,24,128]{2,1,0:T(8,128)(2,1)S(1)}, u32[]{:S(2)}, u32[]{:S(2)}) collective-permute-start(bf16[32,24,128]{2,1,0:T(8,128)(2,1)S(1)} %prep.1.own.refs_3_), channel_id=1, source_target_pairs={{0,2},{1,3},{2,0},{3,1},{4,6},{5,7},{6,4},{7,5},{8,10},{9,11},{10,... | collective-permute-start | bytes 589832 | tf_op jit(solution)/shard_map/ppermute | solution.py:387
  12.2 37.4 %collective-permute-start.6 = (bf16[32,24,128]{2,1,0:T(8,128)(2,1)S(1)}, bf16[32,24,128]{2,1,0:T(8,128)(2,1)S(1)}, u32[]{:S(2)}, u32[]{:S(2)}) collective-permute-start(bf16[32,24,128]{2,1,0:T(8,128)(2,1)S(1)} %prep.1.own.refs_3_), channel_id=1, source_target_pairs={{0,1},{1,2},{2,3},{3,0},{4,5},{5,6},{6,7},{7,4},{8,9},{9,10},{10,1... | collective-permute-start | bytes 589832 | tf_op jit(solution)/shard_map/ppermute | solution.py:387
  13.2 13.8 %collective-permute-start.5 = (bf16[32,24,128]{2,1,0:T(8,128)(2,1)S(1)}, bf16[32,24,128]{2,1,0:T(8,128)(2,1)S(1)}, u32[]{:S(2)}, u32[]{:S(2)}) collective-permute-start(bf16[32,24,128]{2,1,0:T(8,128)(2,1)S(1)} %prep.1.own.refs_3_), channel_id=1, source_target_pairs={{16,0},{24,8},{32,16},{40,24},{48,32},{56,40},{64,48},{72,56},{80,... | collective-permute-start | bytes 589832 | tf_op jit(solution)/shard_map/ppermute | solution.py:374
  15.9 22.0 %collective-permute-start.4 = (bf16[32,24,128]{2,1,0:T(8,128)(2,1)S(1)}, bf16[32,24,128]{2,1,0:T(8,128)(2,1)S(1)}, u32[]{:S(2)}, u32[]{:S(2)}) collective-permute-start(bf16[32,24,128]{2,1,0:T(8,128)(2,1)S(1)} %prep.1.own.refs_3_), channel_id=1, source_target_pairs={{8,0},{16,8},{24,16},{32,24},{40,32},{48,40},{56,48},{64,56},{72,6... | collective-permute-start | bytes 589832 | tf_op jit(solution)/shard_map/ppermute | solution.py:374
  18.6 0.7 copy-start.6
  19.3 0.7 copy-start.7
  20.0 0.7 copy-start.8
  27.0 10.7 %collective-permute-start = (bf16[32,24,128]{2,1,0:T(8,128)(2,1)S(1)}, bf16[32,24,128]{2,1,0:T(8,128)(2,1)S(1)}, u32[]{:S(2)}, u32[]{:S(2)}) collective-permute-start(bf16[32,24,128]{2,1,0:T(8,128)(2,1)S(1)} %prep.1.own.refs_3_), channel_id=1, source_target_pairs={{0,4},{1,5},{2,6},{3,7},{4,0},{5,1},{6,2},{7,3},{8,12},{9,13},{10,... | collective-permute-start | bytes 589832 | tf_op jit(solution)/shard_map/ppermute | solution.py:383
  37.7 30.9 %collective-permute-start.3 = (bf16[32,24,128]{2,1,0:T(8,128)(2,1)S(1)}, bf16[32,24,128]{2,1,0:T(8,128)(2,1)S(1)}, u32[]{:S(2)}, u32[]{:S(2)}) collective-permute-start(bf16[32,24,128]{2,1,0:T(8,128)(2,1)S(1)} %collective-permute-done.refs_3_), channel_id=1, source_target_pairs={{0,3},{1,0},{2,1},{3,2},{4,7},{5,4},{6,5},{7,6},{8,11},{9,8},{10,9... | collective-permute-start | bytes 589832 | tf_op jit(solution)/shard_map/ppermute | solution.py:387
  38.0 30.6 %collective-permute-start.2 = (bf16[32,24,128]{2,1,0:T(8,128)(2,1)S(1)}, bf16[32,24,128]{2,1,0:T(8,128)(2,1)S(1)}, u32[]{:S(2)}, u32[]{:S(2)}) collective-permute-start(bf16[32,24,128]{2,1,0:T(8,128)(2,1)S(1)} %collective-permute-done.refs_3_), channel_id=1, source_target_pairs={{0,2},{1,3},{2,0},{3,1},{4,6},{5,7},{6,4},{7,5},{8,10},{9,11},{10,... | collective-permute-start | bytes 589832 | tf_op jit(solution)/shard_map/ppermute | solution.py:387
  45.3 0.7 copy-start.9
  49.5 19.1 %copy-start.11 = (bf16[96,128,128]{2,1,0:T(8,128)(2,1)}, bf16[96,128,128]{2,1,0:T(8,128)(2,1)S(1)}, u32[]{:S(2)}) copy-start(bf16[96,128,128]{2,1,0:T(8,128)(2,1)S(1)} %get-tuple-element.25.refs_8_) | copy-start | bytes 9437188
  49.6 19.1 %collective-permute-start.1 = (bf16[32,24,128]{2,1,0:T(8,128)(2,1)S(1)}, bf16[32,24,128]{2,1,0:T(8,128)(2,1)S(1)}, u32[]{:S(2)}, u32[]{:S(2)}) collective-permute-start(bf16[32,24,128]{2,1,0:T(8,128)(2,1)S(1)} %collective-permute-done.refs_3_), channel_id=1, source_target_pairs={{0,1},{1,2},{2,3},{3,0},{4,5},{5,6},{6,7},{7,4},{8,9},{9,10},{10,1... | collective-permute-start | bytes 589832 | tf_op jit(solution)/shard_map/ppermute | solution.py:387
  68.7 43.8 %copy-start.1 = (f32[16,4096]{1,0:T(8,128)S(1)}, f32[16,4096]{1,0:T(8,128)}, u32[]{:S(2)}) copy-start(f32[16,4096]{1,0:T(8,128)} %refs_9_.1) | copy-start | bytes 786436
  68.7 43.8 %copy-start.3 = (s32[4096]{0:T(1024)S(1)}, s32[4096]{0:T(1024)}, u32[]{:S(2)}) copy-start(s32[4096]{0:T(1024)} %param.10) | copy-start | bytes 49156
  68.7 43.7 %copy-start.10 = (f32[6]{0:T(128)S(1)}, f32[6]{0:T(128)}, u32[]{:S(2)}) copy-start(f32[6]{0:T(128)} %type_hard.1) | copy-start | bytes 76
  76.5 11.1 %collective-permute-start.14 = (bf16[32,16,128]{2,1,0:T(8,128)(2,1)S(1)}, bf16[32,16,128]{2,1,0:T(8,128)(2,1)S(1)}, u32[]{:S(2)}, u32[]{:S(2)}) collective-permute-start(bf16[32,16,128]{2,1,0:T(8,128)(2,1)S(1)} %get-tuple-element.35), channel_id=1, source_target_pairs={{0,1},{1,2},{2,3},{3,0},{4,5},{5,6},{6,7},{7,4},{8,9},{9,10},{10,1... | collective-permute-start | bytes 393224 | tf_op jit(solution)/shard_map/ppermute | solution.py:387
  82.1 7.9 %collective-permute-start.15 = (bf16[32,16,128]{2,1,0:T(8,128)(2,1)S(1)}, bf16[32,16,128]{2,1,0:T(8,128)(2,1)S(1)}, u32[]{:S(2)}, u32[]{:S(2)}) collective-permute-start(bf16[32,16,128]{2,1,0:T(8,128)(2,1)S(1)} %get-tuple-element.36), channel_id=1, source_target_pairs={{0,2},{1,3},{2,0},{3,1},{4,6},{5,7},{6,4},{7,5},{8,10},{9,11},{10,... | collective-permute-start | bytes 393224 | tf_op jit(solution)/shard_map/ppermute | solution.py:387
  82.1 11.4 %collective-permute-start.16 = (bf16[32,16,128]{2,1,0:T(8,128)(2,1)S(1)}, bf16[32,16,128]{2,1,0:T(8,128)(2,1)S(1)}, u32[]{:S(2)}, u32[]{:S(2)}) collective-permute-start(bf16[32,16,128]{2,1,0:T(8,128)(2,1)S(1)} %get-tuple-element.37), channel_id=1, source_target_pairs={{0,3},{1,0},{2,1},{3,2},{4,7},{5,4},{6,5},{7,6},{8,11},{9,8},{10,9... | collective-permute-start | bytes 393224 | tf_op jit(solution)/shard_map/ppermute | solution.py:387
  84.9 17.6 %collective-permute-start.11 = (bf16[32,16,128]{2,1,0:T(8,128)(2,1)S(1)}, bf16[32,16,128]{2,1,0:T(8,128)(2,1)S(1)}, u32[]{:S(2)}, u32[]{:S(2)}) collective-permute-start(bf16[32,16,128]{2,1,0:T(8,128)(2,1)S(1)} %get-tuple-element.31), channel_id=1, source_target_pairs={{0,1},{1,2},{2,3},{3,0},{4,5},{5,6},{6,7},{7,4},{8,9},{9,10},{10,1... | collective-permute-start | bytes 393224 | tf_op jit(solution)/shard_map/ppermute | solution.py:387
  84.9 17.7 %collective-permute-start.12 = (bf16[32,16,128]{2,1,0:T(8,128)(2,1)S(1)}, bf16[32,16,128]{2,1,0:T(8,128)(2,1)S(1)}, u32[]{:S(2)}, u32[]{:S(2)}) collective-permute-start(bf16[32,16,128]{2,1,0:T(8,128)(2,1)S(1)} %get-tuple-element.32), channel_id=1, source_target_pairs={{0,2},{1,3},{2,0},{3,1},{4,6},{5,7},{6,4},{7,5},{8,10},{9,11},{10,... | collective-permute-start | bytes 393224 | tf_op jit(solution)/shard_map/ppermute | solution.py:387
  87.7 14.9 %collective-permute-start.13 = (bf16[32,16,128]{2,1,0:T(8,128)(2,1)S(1)}, bf16[32,16,128]{2,1,0:T(8,128)(2,1)S(1)}, u32[]{:S(2)}, u32[]{:S(2)}) collective-permute-start(bf16[32,16,128]{2,1,0:T(8,128)(2,1)S(1)} %get-tuple-element.33), channel_id=1, source_target_pairs={{0,3},{1,0},{2,1},{3,2},{4,7},{5,4},{6,5},{7,6},{8,11},{9,8},{10,9... | collective-permute-start | bytes 393224 | tf_op jit(solution)/shard_map/ppermute | solution.py:387
  90.0 12.6 %collective-permute-start.9 = (bf16[32,16,128]{2,1,0:T(8,128)(2,1)S(1)}, bf16[32,16,128]{2,1,0:T(8,128)(2,1)S(1)}, u32[]{:S(2)}, u32[]{:S(2)}) collective-permute-start(bf16[32,16,128]{2,1,0:T(8,128)(2,1)S(1)} %get-tuple-element.28), channel_id=1, source_target_pairs={{0,8},{8,16},{16,24},{24,32},{32,40},{40,48},{48,56},{56,64},{64,7... | collective-permute-start | bytes 393224 | tf_op jit(solution)/shard_map/ppermute | solution.py:379
  93.5 12.4 %collective-permute-start.10 = (bf16[32,16,128]{2,1,0:T(8,128)(2,1)S(1)}, bf16[32,16,128]{2,1,0:T(8,128)(2,1)S(1)}, u32[]{:S(2)}, u32[]{:S(2)}) collective-permute-start(bf16[32,16,128]{2,1,0:T(8,128)(2,1)S(1)} %get-tuple-element.29), channel_id=1, source_target_pairs={{0,16},{8,24},{16,32},{24,40},{32,48},{40,56},{48,64},{56,72},{64,... | collective-permute-start | bytes 393224 | tf_op jit(solution)/shard_map/ppermute | solution.py:379
  102.5 9.9 %collective-permute-start.17 = (bf16[32,16,128]{2,1,0:T(8,128)(2,1)S(1)}, bf16[32,16,128]{2,1,0:T(8,128)(2,1)S(1)}, u32[]{:S(2)}, u32[]{:S(2)}) collective-permute-start(bf16[32,16,128]{2,1,0:T(8,128)(2,1)S(1)} %far_sum.1), channel_id=1, source_target_pairs={{0,4},{1,5},{2,6},{3,7},{4,0},{5,1},{6,2},{7,3},{8,12},{9,13},{10,... | collective-permute-start | bytes 393224 | tf_op jit(solution)/shard_map/ppermute | solution.py:383
where the time goes:
time: 119 us; the launch traced here: 116 us
  starting transfers between devices  46.4 us (39%)
  Pallas kernels  45.8 us (38%)
  waiting for transfers between devices  17 us (14%)
  local copies, waits for them, and re-layouts  5.97 us (5%)
    ppermute x12, starting transfers between devices, around(): lax.ppermute(value, 'col', [(c, (c & 4) + (c + steps) % 4) for c in range...  24.1 us
    pallas_call x1, Pallas kernels, on_device(): call(functools.partial(near_far_kernel, 0), [shape(block_set, F32)] + [sh...  18.9 us
    ppermute x2, starting transfers between devices, passed_up(): lax.ppermute(value, 'row', [(s, s + steps) for s in range(count - steps)])  12.4 us
    ppermute x2, waiting for transfers between devices, across(): return lax.ppermute(value, 'col', [(c, c ^ 4) for c in range(8)])  11.9 us
    pallas_call x1, Pallas kernels, on_device(): call(functools.partial(near_far_kernel, 1), [shape(block_set, BF16)] * 4...  7.82 us
    pallas_call x1, Pallas kernels, on_device(): call(side_kernel, (shape((BLOCKS, BLK), jnp.int32), shape((2 * SLOT_SPAN...  6.29 us
    unnamed x24, local copies, waits for them, and re-layouts  5.97 us
    ppermute x2, starting transfers between devices, across(): return lax.ppermute(value, 'col', [(c, c ^ 4) for c in range(8)])  5.29 us
  transfers between devices with their start and end apart: 18, of which 4 were waited for; matrix products, arithmetic and copies ran while one was open for 0% of the time, Pallas kernels for 25%

commit v1 on v0

--- a/solution.py
+++ b/solution.py
@@ -32,7 +32,14 @@
     0.0005233424709803657,
 )
 
-PAIR_COST = pl.CostEstimate(flops=16_000_000_000, transcendentals=0, bytes_accessed=8_000_000)
+
+def time_cost(microseconds):
+    return pl.CostEstimate(
+        flops=int(microseconds * 1_000_000_000), transcendentals=0, bytes_accessed=1_000_000
+    )
+
+
+PAIR_COST = time_cost(16)
 
 VMEM = pl.BlockSpec(memory_space=pltpu.VMEM)
 SMEM = pl.BlockSpec(memory_space=pltpu.SMEM)
@@ -404,10 +411,9 @@
     )(place, positions, kinds, krylov, order)
 
     other = across(packed)
-    near_rows = [packed] + [around(packed, k) for k in (1, 2, 3)]
     after = passed_down(packed, 1)
     second = passed_down(packed, 2)
-    far_rows = [other] + [around(other, k) for k in (1, 2, 3)]
+    rows_list, _ = lax.optimization_barrier((pair_rows.reshape(-1), packed))
 
     inverse, codes, counts = call(
         side_kernel,
@@ -419,7 +425,10 @@
         [SMEM, SMEM, SMEM, SMEM, VMEM],
         (VMEM, SMEM, SMEM),
         "side",
-    )(place, pair_rows.reshape(-1), pair_cols.reshape(-1), pair_count.reshape(-1), order)
+        cost=time_cost(12),
+    )(place, rows_list, pair_cols.reshape(-1), pair_count.reshape(-1), order)
+
+    near_rows = [packed] + [around(packed, k) for k in (1, 2, 3)]
 
     features, vectors = call(
         feature_kernel,
@@ -427,9 +436,11 @@
         [SMEM, VMEM, VMEM, VMEM],
         (VMEM, VMEM),
         "features",
+        cost=time_cost(5),
     )(type_width, packed, after, second)
 
-    steps = step_tables()
+    far_rows = [other] + [around(other, k) for k in (1, 2, 3)]
+    steps, _ = lax.optimization_barrier((step_tables(), other))
     scratch = [
         pltpu.VMEM((HALF, ROWS, BLK), BF16),
         pltpu.VMEM((HALF + 1, VECS, BLK), F32),
@@ -447,7 +458,6 @@
         scratch=scratch,
         cost=PAIR_COST,
     )(place, counts, codes, *near_rows, vectors, features, steps)
-    near_parts = [near_sums[0]] + [around(near_sums[k], k) for k in (1, 2, 3)]
 
     *far_sums, own_sum, after_sum, last_sum = call(
         functools.partial(near_far_kernel, 1),
@@ -466,6 +476,8 @@
         sum_kernel, shape((BLOCKS, VECS, BLK), BF16), [VMEM] * 4, VMEM, "far_sum"
     )(*far_parts)
     from_far = across(far_sum)
+    near_sums, _ = lax.optimization_barrier((near_sums, far_sum))
+    near_parts = [near_sums[0]] + [around(near_sums[k], k) for k in (1, 2, 3)]
 
     parts = [own_sum, from_prior, from_second, *near_parts, from_far]
     return call(

time: 119 us -> 110 us (0.924)
  the two profiles are of different devices: /device:TPU:6 before, /device:TPU:5 now
where the time goes in v1:
time: 110 us
  Pallas kernels  46.4 us (42%)
  starting transfers between devices  45.5 us (41%)
  waiting for transfers between devices  11.5 us (10%)
  local copies, waits for them, and re-layouts  5.32 us (5%)
    pallas_call x1, Pallas kernels, on_device(): call(functools.partial(near_far_kernel, 0), [shape(block_set, F32)] + [sh...  20.3 us
    ppermute x12, starting transfers between devices, around(): lax.ppermute(value, 'col', [(c, (c & 4) + (c + steps) % 4) for c in range...  14.6 us
    ppermute x2, starting transfers between devices, across(): return lax.ppermute(value, 'col', [(c, c ^ 4) for c in range(8)])  14.1 us
    ppermute x2, starting transfers between devices, passed_up(): lax.ppermute(value, 'row', [(s, s + steps) for s in range(count - steps)])  11.2 us
    pallas_call x1, Pallas kernels, on_device(): call(functools.partial(near_far_kernel, 1), [shape(block_set, BF16)] * 4...  6.88 us
    ppermute x2, waiting for transfers between devices, across(): return lax.ppermute(value, 'col', [(c, c ^ 4) for c in range(8)])  6.73 us
    pallas_call x1, Pallas kernels, on_device(): call(side_kernel, (shape((BLOCKS, BLK), jnp.int32), shape((2 * SLOT_SPAN...  6.38 us
    ppermute x2, starting transfers between devices, passed_down(): lax.ppermute(value, 'row', [(s, s - steps) for s in range(steps, count)])  5.57 us
  transfers between devices with their start and end apart: 18, of which 2 were waited for; matrix products, arithmetic and copies ran while one was open for 0% of the time, Pallas kernels for 28%

profile of v1, /device:TPU:5, one launch (start us, length us, event | category | flops | bytes accessed | tf_op | source)
XLA Modules:
  0.0 109.9 jit_solution(10714890130888251668)
XLA Ops:
  0.1 0.9 copy-done
  1.0 0.7 copy-done.2
  1.7 0.8 copy-done.4
  2.6 0.7 copy-done.5
  3.3 5.2 %prep.1.own.refs_3_ = bf16[32,24,128]{2,1,0:T(8,128)(2,1)S(1)} custom-call(s32[2]{0:T(128)S(1)} %pad_add_fusion.place.refs_0_, f32[3,4096]{1,0:T(4,128)S(1)} %copy-done.4, s32[1,4096]{1,0:T(1,128)S(1)} %bitcast.8, f32[16,4096]{1,0:T(8,128)S(1)} %copy-done, s32[32,128]{1,0:T(8,128)S(1)} %bitcast.10), custom_call_target="tpu_custom_call" | custom-call | tf_op jit(solution)/shard_map/prep/pallas_call | solution.py:404
  8.5 2.8 %collective-permute-start.8 = (bf16[32,24,128]{2,1,0:T(8,128)(2,1)S(1)}, bf16[32,24,128]{2,1,0:T(8,128)(2,1)S(1)}, u32[]{:S(2)}, u32[]{:S(2)}) collective-permute-start(bf16[32,24,128]{2,1,0:T(8,128)(2,1)S(1)} %prep.1.own.refs_3_), channel_id=1, source_target_pairs={{0,3},{1,0},{2,1},{3,2},{4,7},{5,4},{6,5},{7,6},{8,11},{9,8},{10,9... | collective-permute-start | bytes 589832 | tf_op jit(solution)/shard_map/ppermute | solution.py:394
  11.3 0.3 collective-permute-start.7
  11.7 2.2 %collective-permute-start.5 = (bf16[32,24,128]{2,1,0:T(8,128)(2,1)S(1)}, bf16[32,24,128]{2,1,0:T(8,128)(2,1)S(1)}, u32[]{:S(2)}, u32[]{:S(2)}) collective-permute-start(bf16[32,24,128]{2,1,0:T(8,128)(2,1)S(1)} %prep.1.own.refs_3_), channel_id=1, source_target_pairs={{16,0},{24,8},{32,16},{40,24},{48,32},{56,40},{64,48},{72,56},{80,... | collective-permute-start | bytes 589832 | tf_op jit(solution)/shard_map/ppermute | solution.py:381
  13.8 3.4 %collective-permute-start.4 = (bf16[32,24,128]{2,1,0:T(8,128)(2,1)S(1)}, bf16[32,24,128]{2,1,0:T(8,128)(2,1)S(1)}, u32[]{:S(2)}, u32[]{:S(2)}) collective-permute-start(bf16[32,24,128]{2,1,0:T(8,128)(2,1)S(1)} %prep.1.own.refs_3_), channel_id=1, source_target_pairs={{8,0},{16,8},{24,16},{32,24},{40,32},{48,40},{56,48},{64,56},{72,6... | collective-permute-start | bytes 589832 | tf_op jit(solution)/shard_map/ppermute | solution.py:381
  17.3 7.0 %collective-permute-start = (bf16[32,24,128]{2,1,0:T(8,128)(2,1)S(1)}, bf16[32,24,128]{2,1,0:T(8,128)(2,1)S(1)}, u32[]{:S(2)}, u32[]{:S(2)}) collective-permute-start(bf16[32,24,128]{2,1,0:T(8,128)(2,1)S(1)} %prep.1.own.refs_3_), channel_id=1, source_target_pairs={{0,4},{1,5},{2,6},{3,7},{4,0},{5,1},{6,2},{7,3},{8,12},{9,13},{10,... | collective-permute-start | bytes 589832 | tf_op jit(solution)/shard_map/ppermute | solution.py:390
  25.0 0.7 copy-done.6
  25.7 0.7 copy-done.8
  26.4 0.7 copy-done.9
  27.1 6.4 %side.1 = (s32[32,128]{1,0:T(8,128)S(1)}, s32[1041]{0:T(1024)S(1)}, s32[2]{0:T(128)S(1)}) custom-call(s32[2]{0:T(128)S(1)} %pad_add_fusion.place.refs_0_, s32[512]{0:T(512)S(1)} %bitcast.12, s32[512]{0:T(512)S(1)} %bitcast.13, s32[1]{0:T(128)} %bitcast.7.count, s32[32,128]{1,0:T(8,128)S(1)} %bitcast.11), custom_call_target="tpu_custom_call" | custom-call | flops 12000000000 | bytes 1000000 | tf_op jit(solution)/shard_map/side/pallas_call | solution.py:418
  33.4 0.2 select_select_fusion.refs_9_
  33.6 1.6 %collective-permute-start.6 = (bf16[32,24,128]{2,1,0:T(8,128)(2,1)S(1)}, bf16[32,24,128]{2,1,0:T(8,128)(2,1)S(1)}, u32[]{:S(2)}, u32[]{:S(2)}) collective-permute-start(bf16[32,24,128]{2,1,0:T(8,128)(2,1)S(1)} %prep.1.own.refs_3_), channel_id=1, source_target_pairs={{0,1},{1,2},{2,3},{3,0},{4,5},{5,6},{6,7},{7,4},{8,9},{9,10},{10,1... | collective-permute-start | bytes 589832 | tf_op jit(solution)/shard_map/ppermute | solution.py:394
  35.3 1.1 %collective-permute-start.3 = (bf16[32,24,128]{2,1,0:T(8,128)(2,1)S(1)}, bf16[32,24,128]{2,1,0:T(8,128)(2,1)S(1)}, u32[]{:S(2)}, u32[]{:S(2)}) collective-permute-start(bf16[32,24,128]{2,1,0:T(8,128)(2,1)S(1)} %collective-permute-done.refs_3_), channel_id=1, source_target_pairs={{0,3},{1,0},{2,1},{3,2},{4,7},{5,4},{6,5},{7,6},{8,11},{9,8},{10,9... | collective-permute-start | bytes 589832 | tf_op jit(solution)/shard_map/ppermute | solution.py:394
  36.4 0.8 collective-permute-start.2
  37.2 3.6 %features.1 = (bf16[96,128,128]{2,1,0:T(8,128)(2,1)S(1)}, bf16[96,16,128]{2,1,0:T(8,128)(2,1)S(1)}) custom-call(f32[6]{0:T(128)S(1)} %copy-done.10, bf16[32,24,128]{2,1,0:T(8,128)(2,1)S(1)} %prep.1.own.refs_3_, bf16[32,24,128]{2,1,0:T(8,128)(2,1)S(1)} %collective-permute-done.4.after, bf16[32,24,128]{2,1,0:T(8,128)(2,1)S(1)} %collective-permute-done.5.second), custom_call_target="tpu_custom_call" | custom-call | flops 5000000000 | bytes 1000000 | tf_op jit(solution)/shard_map/features/pallas_call | solution.py:433
  40.9 4.8 %collective-permute-done.6.refs_4_ = bf16[32,24,128]{2,1,0:T(8,128)(2,1)S(1)} collective-permute-done((bf16[32,24,128]{2,1,0:T(8,128)(2,1)S(1)}, bf16[32,24,128]{2,1,0:T(8,128)(2,1)S(1)}, u32[]{:S(2)}, u32[]{:S(2)}) %collective-permute-start.6) | collective-permute-done | bytes 196640 | tf_op jit(solution)/shard_map/ppermute | solution.py:394
  45.6 20.3 %pairs_near.1 = (f32[32,16,128]{2,1,0:T(8,128)S(1)}, bf16[32,16,128]{2,1,0:T(8,128)(2,1)S(1)}, bf16[32,16,128]{2,1,0:T(8,128)(2,1)S(1)}, bf16[32,16,128]{2,1,0:T(8,128)(2,1)S(1)}, f32[96,16,128]{2,1,0:T(8,128)S(1)}) custom-call(s32[2]{0:T(128)S(1)} %pad_add_fusion.place.refs_0_, s32[2]{0:T(128)S(1)} %get-tuple-element.29.refs_1_, ...), custom_call_target="tpu_custom_call" | custom-call | flops 16000000000 | bytes 1000000 | tf_op jit(solution)/shard_map/pairs_near/pallas_call | solution.py:452
  66.0 6.9 %pairs_far.1 = (bf16[32,16,128]{2,1,0:T(8,128)(2,1)S(1)}, bf16[32,16,128]{2,1,0:T(8,128)(2,1)S(1)}, bf16[32,16,128]{2,1,0:T(8,128)(2,1)S(1)}, bf16[32,16,128]{2,...) custom-call(s32[2]{0:T(128)S(1)} %pad_add_fusion.place.refs_0_, ...), custom_call_target="tpu_custom_call" | custom-call | flops 16000000000 | bytes 1000000 | tf_op jit(solution)/shard_map/pairs_far/pallas_call | solution.py:462
  72.9 0.9 collective-permute-start.11
  73.8 2.5 %collective-permute-start.13 = (bf16[32,16,128]{2,1,0:T(8,128)(2,1)S(1)}, bf16[32,16,128]{2,1,0:T(8,128)(2,1)S(1)}, u32[]{:S(2)}, u32[]{:S(2)}) collective-permute-start(bf16[32,16,128]{2,1,0:T(8,128)(2,1)S(1)} %get-tuple-element.45), channel_id=1, source_target_pairs={{0,3},{1,0},{2,1},{3,2},{4,7},{5,4},{6,5},{7,6},{8,11},{9,8},{10,9... | collective-permute-start | bytes 393224 | tf_op jit(solution)/shard_map/ppermute | solution.py:394
  76.3 9.0 %collective-permute-start.9 = (bf16[32,16,128]{2,1,0:T(8,128)(2,1)S(1)}, bf16[32,16,128]{2,1,0:T(8,128)(2,1)S(1)}, u32[]{:S(2)}, u32[]{:S(2)}) collective-permute-start(bf16[32,16,128]{2,1,0:T(8,128)(2,1)S(1)} %get-tuple-element.36), channel_id=1, source_target_pairs={{0,8},{8,16},{16,24},{24,32},{32,40},{40,48},{48,56},{56,64},{64,7... | collective-permute-start | bytes 393224 | tf_op jit(solution)/shard_map/ppermute | solution.py:386
  85.3 2.2 %collective-permute-start.10 = (bf16[32,16,128]{2,1,0:T(8,128)(2,1)S(1)}, bf16[32,16,128]{2,1,0:T(8,128)(2,1)S(1)}, u32[]{:S(2)}, u32[]{:S(2)}) collective-permute-start(bf16[32,16,128]{2,1,0:T(8,128)(2,1)S(1)} %get-tuple-element.37), channel_id=1, source_target_pairs={{0,16},{8,24},{16,32},{24,40},{32,48},{40,56},{48,64},{56,72},{64,... | collective-permute-start | bytes 393224 | tf_op jit(solution)/shard_map/ppermute | solution.py:386
  87.6 0.4 collective-permute-start.14
  88.0 2.2 %collective-permute-start.15 = (bf16[32,16,128]{2,1,0:T(8,128)(2,1)S(1)}, bf16[32,16,128]{2,1,0:T(8,128)(2,1)S(1)}, u32[]{:S(2)}, u32[]{:S(2)}) collective-permute-start(bf16[32,16,128]{2,1,0:T(8,128)(2,1)S(1)} %get-tuple-element.48), channel_id=1, source_target_pairs={{0,2},{1,3},{2,0},{3,1},{4,6},{5,7},{6,4},{7,5},{8,10},{9,11},{10,... | collective-permute-start | bytes 393224 | tf_op jit(solution)/shard_map/ppermute | solution.py:394
  90.1 2.0 %collective-permute-start.16 = (bf16[32,16,128]{2,1,0:T(8,128)(2,1)S(1)}, bf16[32,16,128]{2,1,0:T(8,128)(2,1)S(1)}, u32[]{:S(2)}, u32[]{:S(2)}) collective-permute-start(bf16[32,16,128]{2,1,0:T(8,128)(2,1)S(1)} %get-tuple-element.49), channel_id=1, source_target_pairs={{0,3},{1,0},{2,1},{3,2},{4,7},{5,4},{6,5},{7,6},{8,11},{9,8},{10,9... | collective-permute-start | bytes 393224 | tf_op jit(solution)/shard_map/ppermute | solution.py:394
  92.1 7.1 %collective-permute-start.17 = (bf16[32,16,128]{2,1,0:T(8,128)(2,1)S(1)}, bf16[32,16,128]{2,1,0:T(8,128)(2,1)S(1)}, u32[]{:S(2)}, u32[]{:S(2)}) collective-permute-start(bf16[32,16,128]{2,1,0:T(8,128)(2,1)S(1)} %far_sum.1), channel_id=1, source_target_pairs={{0,4},{1,5},{2,6},{3,7},{4,0},{5,1},{6,2},{7,3},{8,12},{9,13},{10,... | collective-permute-start | bytes 393224 | tf_op jit(solution)/shard_map/ppermute | solution.py:390
  99.3 6.7 %collective-permute-done.17.refs_7_ = bf16[32,16,128]{2,1,0:T(8,128)(2,1)S(1)} collective-permute-done((bf16[32,16,128]{2,1,0:T(8,128)(2,1)S(1)}, bf16[32,16,128]{2,1,0:T(8,128)(2,1)S(1)}, u32[]{:S(2)}, u32[]{:S(2)}) %collective-permute-start.17) | collective-permute-done | bytes 131104 | tf_op jit(solution)/shard_map/ppermute | solution.py:390
  106.0 3.9 %final.1 = f32[16,4096]{1,0:T(8,128)} custom-call(f32[6]{0:T(128)S(1)} %copy-done.7, f32[32,16,128]{2,1,0:T(8,128)S(1)} %get-tuple-element.35.refs_0_, bf16[32,16,128]{2,1,0:T(8,128)(2,1)S(1)} %collective-permute-done.9.refs_1_, bf16[32,16,128]{2,1,0:T(8,128)(2,1)S(1)} %collective-permute-done.10.refs_2_, f32[32,16,128]{2,1,0:T(8,128)S(1)} %get-tuple-element.46.refs_3_, ...), custom_call_target="tpu_custom_call" | custom-call | tf_op jit(solution)/shard_map/final/pallas_call | solution.py:483
  (43 shorter events, 0.3 us)
Async XLA Ops:
  0.1 0.9 copy-start
  1.0 0.7 copy-start.2
  1.7 0.8 copy-start.4
  2.6 0.7 copy-start.5
  8.5 32.2 %collective-permute-start.8 = (bf16[32,24,128]{2,1,0:T(8,128)(2,1)S(1)}, bf16[32,24,128]{2,1,0:T(8,128)(2,1)S(1)}, u32[]{:S(2)}, u32[]{:S(2)}) collective-permute-start(bf16[32,24,128]{2,1,0:T(8,128)(2,1)S(1)} %prep.1.own.refs_3_), channel_id=1, source_target_pairs={{0,3},{1,0},{2,1},{3,2},{4,7},{5,4},{6,5},{7,6},{8,11},{9,8},{10,9... | collective-permute-start | bytes 589832 | tf_op jit(solution)/shard_map/ppermute | solution.py:394
  11.3 29.5 %collective-permute-start.7 = (bf16[32,24,128]{2,1,0:T(8,128)(2,1)S(1)}, bf16[32,24,128]{2,1,0:T(8,128)(2,1)S(1)}, u32[]{:S(2)}, u32[]{:S(2)}) collective-permute-start(bf16[32,24,128]{2,1,0:T(8,128)(2,1)S(1)} %prep.1.own.refs_3_), channel_id=1, source_target_pairs={{0,2},{1,3},{2,0},{3,1},{4,6},{5,7},{6,4},{7,5},{8,10},{9,11},{10,... | collective-permute-start | bytes 589832 | tf_op jit(solution)/shard_map/ppermute | solution.py:394
  11.7 23.6 %collective-permute-start.5 = (bf16[32,24,128]{2,1,0:T(8,128)(2,1)S(1)}, bf16[32,24,128]{2,1,0:T(8,128)(2,1)S(1)}, u32[]{:S(2)}, u32[]{:S(2)}) collective-permute-start(bf16[32,24,128]{2,1,0:T(8,128)(2,1)S(1)} %prep.1.own.refs_3_), channel_id=1, source_target_pairs={{16,0},{24,8},{32,16},{40,24},{48,32},{56,40},{64,48},{72,56},{80,... | collective-permute-start | bytes 589832 | tf_op jit(solution)/shard_map/ppermute | solution.py:381
  13.8 22.5 %collective-permute-start.4 = (bf16[32,24,128]{2,1,0:T(8,128)(2,1)S(1)}, bf16[32,24,128]{2,1,0:T(8,128)(2,1)S(1)}, u32[]{:S(2)}, u32[]{:S(2)}) collective-permute-start(bf16[32,24,128]{2,1,0:T(8,128)(2,1)S(1)} %prep.1.own.refs_3_), channel_id=1, source_target_pairs={{8,0},{16,8},{24,16},{32,24},{40,32},{48,40},{56,48},{64,56},{72,6... | collective-permute-start | bytes 589832 | tf_op jit(solution)/shard_map/ppermute | solution.py:381
  17.3 16.3 %collective-permute-start = (bf16[32,24,128]{2,1,0:T(8,128)(2,1)S(1)}, bf16[32,24,128]{2,1,0:T(8,128)(2,1)S(1)}, u32[]{:S(2)}, u32[]{:S(2)}) collective-permute-start(bf16[32,24,128]{2,1,0:T(8,128)(2,1)S(1)} %prep.1.own.refs_3_), channel_id=1, source_target_pairs={{0,4},{1,5},{2,6},{3,7},{4,0},{5,1},{6,2},{7,3},{8,12},{9,13},{10,... | collective-permute-start | bytes 589832 | tf_op jit(solution)/shard_map/ppermute | solution.py:390
  25.0 0.7 copy-start.6
  25.7 0.7 copy-start.8
  26.4 0.7 copy-start.9
  27.1 10.1 %copy-start.10 = (f32[6]{0:T(128)S(1)}, f32[6]{0:T(128)}, u32[]{:S(2)}) copy-start(f32[6]{0:T(128)} %type_width.1) | copy-start | bytes 76
  33.6 12.0 %collective-permute-start.6 = (bf16[32,24,128]{2,1,0:T(8,128)(2,1)S(1)}, bf16[32,24,128]{2,1,0:T(8,128)(2,1)S(1)}, u32[]{:S(2)}, u32[]{:S(2)}) collective-permute-start(bf16[32,24,128]{2,1,0:T(8,128)(2,1)S(1)} %prep.1.own.refs_3_), channel_id=1, source_target_pairs={{0,1},{1,2},{2,3},{3,0},{4,5},{5,6},{6,7},{7,4},{8,9},{9,10},{10,1... | collective-permute-start | bytes 589832 | tf_op jit(solution)/shard_map/ppermute | solution.py:394
  35.3 30.7 %collective-permute-start.3 = (bf16[32,24,128]{2,1,0:T(8,128)(2,1)S(1)}, bf16[32,24,128]{2,1,0:T(8,128)(2,1)S(1)}, u32[]{:S(2)}, u32[]{:S(2)}) collective-permute-start(bf16[32,24,128]{2,1,0:T(8,128)(2,1)S(1)} %collective-permute-done.refs_3_), channel_id=1, source_target_pairs={{0,3},{1,0},{2,1},{3,2},{4,7},{5,4},{6,5},{7,6},{8,11},{9,8},{10,9... | collective-permute-start | bytes 589832 | tf_op jit(solution)/shard_map/ppermute | solution.py:394
  36.4 29.6 %collective-permute-start.2 = (bf16[32,24,128]{2,1,0:T(8,128)(2,1)S(1)}, bf16[32,24,128]{2,1,0:T(8,128)(2,1)S(1)}, u32[]{:S(2)}, u32[]{:S(2)}) collective-permute-start(bf16[32,24,128]{2,1,0:T(8,128)(2,1)S(1)} %collective-permute-done.refs_3_), channel_id=1, source_target_pairs={{0,2},{1,3},{2,0},{3,1},{4,6},{5,7},{6,4},{7,5},{8,10},{9,11},{10,... | collective-permute-start | bytes 589832 | tf_op jit(solution)/shard_map/ppermute | solution.py:394
  40.8 25.2 %copy-start.11 = (bf16[96,128,128]{2,1,0:T(8,128)(2,1)}, bf16[96,128,128]{2,1,0:T(8,128)(2,1)S(1)}, u32[]{:S(2)}) copy-start(bf16[96,128,128]{2,1,0:T(8,128)(2,1)S(1)} %get-tuple-element.32.refs_8_) | copy-start | bytes 9437188
  40.8 25.2 %collective-permute-start.1 = (bf16[32,24,128]{2,1,0:T(8,128)(2,1)S(1)}, bf16[32,24,128]{2,1,0:T(8,128)(2,1)S(1)}, u32[]{:S(2)}, u32[]{:S(2)}) collective-permute-start(bf16[32,24,128]{2,1,0:T(8,128)(2,1)S(1)} %collective-permute-done.refs_3_), channel_id=1, source_target_pairs={{0,1},{1,2},{2,3},{3,0},{4,5},{5,6},{6,7},{7,4},{8,9},{9,10},{10,1... | collective-permute-start | bytes 589832 | tf_op jit(solution)/shard_map/ppermute | solution.py:394
  66.0 40.0 %copy-start.1 = (f32[16,4096]{1,0:T(8,128)S(1)}, f32[16,4096]{1,0:T(8,128)}, u32[]{:S(2)}) copy-start(f32[16,4096]{1,0:T(8,128)} %refs_9_.1) | copy-start | bytes 786436
  66.0 40.0 %copy-start.3 = (s32[4096]{0:T(1024)S(1)}, s32[4096]{0:T(1024)}, u32[]{:S(2)}) copy-start(s32[4096]{0:T(1024)} %param.10) | copy-start | bytes 49156
  66.0 40.0 %copy-start.7 = (f32[6]{0:T(128)S(1)}, f32[6]{0:T(128)}, u32[]{:S(2)}) copy-start(f32[6]{0:T(128)} %type_hard.1) | copy-start | bytes 76
  72.9 14.6 %collective-permute-start.11 = (bf16[32,16,128]{2,1,0:T(8,128)(2,1)S(1)}, bf16[32,16,128]{2,1,0:T(8,128)(2,1)S(1)}, u32[]{:S(2)}, u32[]{:S(2)}) collective-permute-start(bf16[32,16,128]{2,1,0:T(8,128)(2,1)S(1)} %get-tuple-element.43), channel_id=1, source_target_pairs={{0,1},{1,2},{2,3},{3,0},{4,5},{5,6},{6,7},{7,4},{8,9},{9,10},{10,1... | collective-permute-start | bytes 393224 | tf_op jit(solution)/shard_map/ppermute | solution.py:394
  73.8 13.7 %collective-permute-start.12 = (bf16[32,16,128]{2,1,0:T(8,128)(2,1)S(1)}, bf16[32,16,128]{2,1,0:T(8,128)(2,1)S(1)}, u32[]{:S(2)}, u32[]{:S(2)}) collective-permute-start(bf16[32,16,128]{2,1,0:T(8,128)(2,1)S(1)} %get-tuple-element.44), channel_id=1, source_target_pairs={{0,2},{1,3},{2,0},{3,1},{4,6},{5,7},{6,4},{7,5},{8,10},{9,11},{10,... | collective-permute-start | bytes 393224 | tf_op jit(solution)/shard_map/ppermute | solution.py:394
  73.8 13.7 %collective-permute-start.13 = (bf16[32,16,128]{2,1,0:T(8,128)(2,1)S(1)}, bf16[32,16,128]{2,1,0:T(8,128)(2,1)S(1)}, u32[]{:S(2)}, u32[]{:S(2)}) collective-permute-start(bf16[32,16,128]{2,1,0:T(8,128)(2,1)S(1)} %get-tuple-element.45), channel_id=1, source_target_pairs={{0,3},{1,0},{2,1},{3,2},{4,7},{5,4},{6,5},{7,6},{8,11},{9,8},{10,9... | collective-permute-start | bytes 393224 | tf_op jit(solution)/shard_map/ppermute | solution.py:394
  76.3 15.8 %collective-permute-start.9 = (bf16[32,16,128]{2,1,0:T(8,128)(2,1)S(1)}, bf16[32,16,128]{2,1,0:T(8,128)(2,1)S(1)}, u32[]{:S(2)}, u32[]{:S(2)}) collective-permute-start(bf16[32,16,128]{2,1,0:T(8,128)(2,1)S(1)} %get-tuple-element.36), channel_id=1, source_target_pairs={{0,8},{8,16},{16,24},{24,32},{32,40},{40,48},{48,56},{56,64},{64,7... | collective-permute-start | bytes 393224 | tf_op jit(solution)/shard_map/ppermute | solution.py:386
  85.3 14.0 %collective-permute-start.10 = (bf16[32,16,128]{2,1,0:T(8,128)(2,1)S(1)}, bf16[32,16,128]{2,1,0:T(8,128)(2,1)S(1)}, u32[]{:S(2)}, u32[]{:S(2)}) collective-permute-start(bf16[32,16,128]{2,1,0:T(8,128)(2,1)S(1)} %get-tuple-element.37), channel_id=1, source_target_pairs={{0,16},{8,24},{16,32},{24,40},{32,48},{40,56},{48,64},{56,72},{64,... | collective-permute-start | bytes 393224 | tf_op jit(solution)/shard_map/ppermute | solution.py:386
  87.6 11.6 %collective-permute-start.14 = (bf16[32,16,128]{2,1,0:T(8,128)(2,1)S(1)}, bf16[32,16,128]{2,1,0:T(8,128)(2,1)S(1)}, u32[]{:S(2)}, u32[]{:S(2)}) collective-permute-start(bf16[32,16,128]{2,1,0:T(8,128)(2,1)S(1)} %get-tuple-element.47), channel_id=1, source_target_pairs={{0,1},{1,2},{2,3},{3,0},{4,5},{5,6},{6,7},{7,4},{8,9},{9,10},{10,1... | collective-permute-start | bytes 393224 | tf_op jit(solution)/shard_map/ppermute | solution.py:394
  88.0 11.3 %collective-permute-start.15 = (bf16[32,16,128]{2,1,0:T(8,128)(2,1)S(1)}, bf16[32,16,128]{2,1,0:T(8,128)(2,1)S(1)}, u32[]{:S(2)}, u32[]{:S(2)}) collective-permute-start(bf16[32,16,128]{2,1,0:T(8,128)(2,1)S(1)} %get-tuple-element.48), channel_id=1, source_target_pairs={{0,2},{1,3},{2,0},{3,1},{4,6},{5,7},{6,4},{7,5},{8,10},{9,11},{10,... | collective-permute-start | bytes 393224 | tf_op jit(solution)/shard_map/ppermute | solution.py:394
  90.1 9.1 %collective-permute-start.16 = (bf16[32,16,128]{2,1,0:T(8,128)(2,1)S(1)}, bf16[32,16,128]{2,1,0:T(8,128)(2,1)S(1)}, u32[]{:S(2)}, u32[]{:S(2)}) collective-permute-start(bf16[32,16,128]{2,1,0:T(8,128)(2,1)S(1)} %get-tuple-element.49), channel_id=1, source_target_pairs={{0,3},{1,0},{2,1},{3,2},{4,7},{5,4},{6,5},{7,6},{8,11},{9,8},{10,9... | collective-permute-start | bytes 393224 | tf_op jit(solution)/shard_map/ppermute | solution.py:394
  92.1 13.9 %collective-permute-start.17 = (bf16[32,16,128]{2,1,0:T(8,128)(2,1)S(1)}, bf16[32,16,128]{2,1,0:T(8,128)(2,1)S(1)}, u32[]{:S(2)}, u32[]{:S(2)}) collective-permute-start(bf16[32,16,128]{2,1,0:T(8,128)(2,1)S(1)} %far_sum.1), channel_id=1, source_target_pairs={{0,4},{1,5},{2,6},{3,7},{4,0},{5,1},{6,2},{7,3},{8,12},{9,13},{10,... | collective-permute-start | bytes 393224 | tf_op jit(solution)/shard_map/ppermute | solution.py:390

commit v2 on v1

--- a/solution.py
+++ b/solution.py
@@ -2,6 +2,8 @@
 
 import jax
 import jax.numpy as jnp
+import ml_dtypes
+import numpy as np
 from jax import lax
 from jax.experimental import pallas as pl
 from jax.experimental.pallas import tpu as pltpu
@@ -17,19 +19,18 @@
 DEPTH = 80
 UNROLL = 8
 SLOTS = 512
-SLOT_SPAN = SLOTS + UNROLL
+SLOT_SPAN = SLOTS + BLK
+SPARE = 3 << 22
 CELL = (11.0, 5.0, 11.0)
 BOX = (44.0, 30.0, 44.0)
 SOFTENING = 0.5
 
 ERF_COEFFS = (
-    1.1283815681128107,
-    -7.621837438329706e-05,
-    0.10341113638200404,
-    -0.002217632183960096,
-    0.003526363187890101,
-    -0.0031284691084128495,
-    0.0005233424709803657,
+    1.1283733798353786,
+    0.10285896471421105,
+    -0.0004149336902342856,
+    -0.00044422084313997635,
+    3.52820399232984e-05,
 )
 
 
@@ -43,6 +44,7 @@
 
 VMEM = pl.BlockSpec(memory_space=pltpu.VMEM)
 SMEM = pl.BlockSpec(memory_space=pltpu.SMEM)
+ANY = pl.BlockSpec(memory_space=pl.ANY)
 Y_GROUPS = [[0, 1, 2, 3], [4, 5, 6, 7]]
 F32 = jnp.float32
 BF16 = jnp.bfloat16
@@ -63,7 +65,24 @@
     return jnp.take_along_axis(source, index, axis=1, mode="promise_in_bounds")
 
 
-def prep_kernel(place, positions, atom_type, krylov, order, packed, geometry):
+def prep_kernel(
+    place, positions_hbm, type_hbm, krylov_hbm, order_hbm, packed, geometry, positions, atom_type, krylov, order, done
+):
+    loads = [
+        pltpu.make_async_copy(source, target, done.at[k])
+        for k, (source, target) in enumerate(
+            (
+                (krylov_hbm, krylov),
+                (positions_hbm, positions),
+                (type_hbm, atom_type),
+                (order_hbm, order),
+            )
+        )
+    ]
+    for load in loads:
+        load.start()
+    for load in loads:
+        load.wait()
     geometry[...] = jnp.zeros_like(geometry)
     geometry[0:3, :] = positions[...]
     geometry[3:4, :] = atom_type[...].astype(F32)
@@ -99,56 +118,72 @@
     lax.fori_loop(0, BLOCKS, one_block, 0)
 
 
-def side_kernel(place, rows, cols, count, order, inverse, codes, counts):
-    row_index = place[0]
-    col_index = place[1]
-    own_half = col_index >> 2
-
-    live = count[0]
-
-    def some_slots(turn, seen):
-        first, second = seen
-        for extra in range(4):
-            slot = turn * 4 + extra
-            row = rows[slot]
-            col = cols[slot] - row_index * BLOCKS
-            same = (row >> 7) == own_half
-            diagonal = jnp.logical_and(col < BLOCKS, row == col_index * BLOCKS + col)
-            code = (
-                (row & 127)
-                | (col << 7)
-                | ((col_index - (row >> 5) + 4) << 14)
-                | (((col & 31) - (row & 31) + 2) << 18)
-                | (diagonal.astype(jnp.int32) << 21)
-            )
-            used = slot < live
-            target = jnp.where(same, first, SLOT_SPAN + second)
-            codes[jnp.where(used, target, 2 * SLOT_SPAN)] = code
-            one = jnp.logical_and(used, same).astype(jnp.int32)
-            second = second + used.astype(jnp.int32) - one
-            first = first + one
-        return first, second
-
-    first, second = lax.fori_loop(0, (live + 3) // 4, some_slots, (jnp.int32(0), jnp.int32(0)))
-    spare = (4 << 14) | (2 << 18) | (1 << 21) | (1 << 22)
-    for extra in range(UNROLL):
-        codes[first + extra] = spare
-        codes[SLOT_SPAN + second + extra] = spare
-    counts[0] = first
-    counts[1] = second
+def side_kernel(place, count, rows, cols, order, inverse, codes, counts):
+    row = rows[...]
+    col = cols[...] - place[0] * BLOCKS
+    step_y = place[1] - (row >> 5) + 4
+    step_z = (col & 31) - (row & 31) + 2
+    step = ((col >> 5) * 9 + step_y) * 5 + step_z
+    diagonal = jnp.logical_and(col < BLOCKS, row == place[1] * BLOCKS + col)
+    code = (row & 127) | (col << 7) | (step << 14) | (diagonal.astype(jnp.int32) << 22)
+    live = lax.broadcasted_iota(jnp.int32, (1, SLOTS), 1) < count[0]
+    same = (row >> 7) == (place[1] >> 2)
+    near = jnp.logical_and(live, same).astype(F32)
+    far = jnp.logical_and(live, jnp.logical_not(same)).astype(F32)
+    level = lax.broadcasted_iota(jnp.int32, (8, SLOTS), 0)
+    wide = lambda v: jnp.broadcast_to(v, (8, SLOTS))
+    flags = jnp.where(level == 0, wide(near), jnp.where(level == 1, wide(far), 0.0)).astype(BF16)
+    earlier = (
+        (lax.broadcasted_iota(jnp.int32, (SLOTS, SLOTS), 0) < lax.broadcasted_iota(jnp.int32, (SLOTS, SLOTS), 1))
+        .astype(F32)
+        .astype(BF16)
+    )
+    ranks = jnp.dot(flags, earlier, preferred_element_type=F32)
+    target = jnp.where(
+        near > 0.5, ranks[0:1], jnp.where(far > 0.5, ranks[1:2] + float(SLOT_SPAN), -1.0)
+    ).astype(jnp.int32)
+    chosen = (
+        (
+            lax.broadcasted_iota(jnp.int32, (2 * SLOT_SPAN, SLOTS), 0)
+            == jnp.broadcast_to(target, (2 * SLOT_SPAN, SLOTS))
+        )
+        .astype(F32)
+        .astype(BF16)
+    )
+    low = wide((code & 255).astype(F32))
+    middle = wide(((code >> 8) & 255).astype(F32))
+    high = wide((code >> 16).astype(F32))
+    parts = jnp.where(level == 0, low, jnp.where(level == 1, middle, jnp.where(level == 2, high, 0.0)))
+    moved = lax.dot_general(
+        parts.astype(BF16), chosen, (((1,), (1,)), ((), ())), preferred_element_type=F32
+    )
+    listed = (moved[0:1] + moved[1:2] * 256.0 + moved[2:3] * 65536.0).astype(jnp.int32)
+    near_count = jnp.sum(near).astype(jnp.int32)
+    far_count = jnp.sum(far).astype(jnp.int32)
+    spot = lax.broadcasted_iota(jnp.int32, (1, 2 * SLOT_SPAN), 1)
+    in_near = spot < SLOT_SPAN
+    used = jnp.where(in_near, spot, spot - SLOT_SPAN) < jnp.where(in_near, near_count, far_count)
+    codes[...] = jnp.where(used, listed, SPARE)
+    counts[0] = near_count
+    counts[1] = far_count
 
     level_h = lax.broadcasted_iota(jnp.int32, (BLOCKS, BLK), 0)
     level_l = lax.broadcasted_iota(jnp.int32, (BLK, BLK), 0)
     lanes = lax.broadcasted_iota(jnp.int32, (BLOCKS, BLK), 1).astype(F32)
-    total = jnp.zeros((2 * BLOCKS, BLK), F32)
+    left = []
+    right = []
     for block in range(BLOCKS):
         wanted = order[block : block + 1, :]
         in_high = (level_h == jnp.broadcast_to(wanted >> 7, (BLOCKS, BLK))).astype(F32)
-        in_low = (level_l == jnp.broadcast_to(wanted & 127, (BLK, BLK))).astype(F32).astype(BF16)
-        left = jnp.concatenate([in_high * float(block), in_high * lanes], axis=0).astype(BF16)
-        total = total + lax.dot_general(
-            left, in_low, (((1,), (1,)), ((), ())), preferred_element_type=F32
-        )
+        in_low = (level_l == jnp.broadcast_to(wanted & 127, (BLK, BLK))).astype(F32)
+        left.append(jnp.concatenate([in_high * float(block), in_high * lanes], axis=0).astype(BF16))
+        right.append(in_low.astype(BF16))
+    total = lax.dot_general(
+        jnp.concatenate(left, axis=1),
+        jnp.concatenate(right, axis=1),
+        (((1,), (1,)), ((), ())),
+        preferred_element_type=F32,
+    )
     inverse[...] = (total[0:BLOCKS] * float(BLK) + total[BLOCKS:]).astype(jnp.int32)
 
 
@@ -159,10 +194,8 @@
         squares = jnp.where(level == t, type_width[t] * type_width[t], squares)
     low3 = level < 3
     low6 = level < 6
-    last = level == 7
     zero = jnp.zeros((8, BLK), F32)
-    ones = jnp.where(low6, 1.0, 0.0)
-    twos = jnp.where(jnp.logical_and(low6, level >= 3), 2.0, 0.0)
+    ones3 = jnp.where(low3, 1.0, 0.0)
 
     for part, source in enumerate((own, after, second)):
 
@@ -182,14 +215,19 @@
             scale = lax.rsqrt(own_square + squares)
             scale_h, scale_m, scale_l = split3(jnp.where(low6, scale, 0.0))
             wide = lambda v: jnp.broadcast_to(v, (8, BLK))
+            weights = jnp.where(
+                level == 0,
+                wide(weight_h),
+                jnp.where(level == 1, wide(weight_m), jnp.where(level == 2, wide(weight_l), 0.0)),
+            )
             stacked = jnp.concatenate(
                 [
-                    jnp.where(low6, coarse, jnp.where(last, wide(weight_h), 0.0)),
-                    jnp.where(low6, fine, jnp.where(last, wide(weight_m), 0.0)),
-                    jnp.where(last, wide(weight_l), ones),
-                    ones,
-                    twos,
-                    twos,
+                    jnp.where(low6, coarse, 0.0),
+                    jnp.where(low6, fine, 0.0),
+                    jnp.where(low6, coded, 1.0),
+                    weights,
+                    ones3,
+                    zero,
                     scale_h,
                     scale_m,
                     scale_l,
@@ -207,35 +245,60 @@
         lax.fori_loop(0, BLOCKS // 4, some_blocks, 0)
 
 
-def pair_operand(code, row_data, steps):
-    coded = row_data[code & 127, VECS:ROWS, :].astype(F32)
-    col = (code >> 7) & 127
-    shift = steps[col >> 5] + steps[3 + ((code >> 14) & 15)] + steps[12 + ((code >> 18) & 7)]
-    near = coded - shift
-    square = near * near
-    cross = near * pltpu.roll(near, 3, 0)
-    square_h = square.astype(BF16).astype(F32)
-    cross_h = cross.astype(BF16).astype(F32)
-    hot = (sublane().astype(F32) == jnp.broadcast_to(coded[6:7], (8, BLK))).astype(F32)
+def row_operands(row_data, operands):
+    level = sublane()
     zero = jnp.zeros((8, BLK), F32)
-    left = jnp.concatenate(
-        [near, near, square_h, square - square_h, cross_h, cross - cross_h, zero, zero, zero, zero],
-        axis=0,
-    ).astype(BF16)
-    right = jnp.concatenate([zero] * 6 + [hot, hot, hot, zero], axis=0).astype(BF16)
-    return jnp.concatenate([left, right], axis=1)
+
+    def some_rows(turn, carry):
+        for extra in range(8):
+            row = turn * 8 + extra
+            coded = row_data[row, VECS:ROWS, :].astype(F32)
+            near = coded + pltpu.roll(coded, 5, 0)
+            square = near * near
+            weight_h, weight_m, weight_l = split3(square[0:1] + square[1:2] + square[2:3])
+            wide = lambda v: jnp.broadcast_to(v, (8, BLK))
+            weights = jnp.where(
+                level == 0,
+                wide(weight_h),
+                jnp.where(level == 1, wide(weight_m), jnp.where(level == 2, wide(weight_l), 0.0)),
+            )
+            hot = (level.astype(F32) == wide(coded[6:7])).astype(F32)
+            operands[row] = jnp.concatenate(
+                [coded, coded, weights, zero, hot, hot, hot, zero], axis=0
+            ).astype(BF16)
+        return carry
+
+    lax.fori_loop(0, HALF // 8, some_rows, 0)
+
+
+def pair_products(code, operands, features, step_rows, step_lanes):
+    step = (code >> 14) & 255
+    right = operands[code & 127]
+    empty = jnp.zeros((48, BLK), BF16)
+    left = features[(code >> 7) & 127].reshape(8, 16, BLK) + step_lanes[step][None]
+    both = jnp.concatenate(
+        [
+            jnp.concatenate([right[0:16], step_rows[step], right[16:32], empty[0:32]], axis=0),
+            jnp.concatenate([empty, right[32:64]], axis=0),
+        ],
+        axis=1,
+    )
+    return jnp.dot(left.reshape(BLK, BLK)[:, 0:DEPTH], both, preferred_element_type=F32)
 
 
 def tile_values(distance2, scale):
     inverse = lax.rsqrt(distance2)
     z = distance2 * inverse * scale
+    square = z * z
     poly = ERF_COEFFS[-1]
     for coefficient in ERF_COEFFS[-2::-1]:
-        poly = poly * z + coefficient
+        poly = poly * square + coefficient
     return (jnp.tanh(poly * z) * inverse).astype(BF16)
 
 
-def pair_loop(phase, counts, codes, row_data, vectors, features, steps, row_acc, col_acc, waiting, tiles):
+def pair_loop(
+    phase, counts, codes, row_data, operands, vectors, features, step_rows, step_lanes, row_acc, col_acc, waiting, tiles
+):
     base = phase * SLOT_SPAN
     batches = (counts[phase] + UNROLL - 1) // UNROLL
 
@@ -244,7 +307,7 @@
         opening = base + jnp.maximum(jnp.minimum(turn, batches - 1), 0) * UNROLL
         sums = []
         for first in range(0, UNROLL, 2):
-            done = [codes[adding + first + k] for k in range(2)]
+            done = [codes[0, adding + first + k] for k in range(2)]
             both = [tiles[first + k] for k in range(2)]
             forward = jnp.dot(
                 jnp.concatenate([vectors[(code >> 7) & 127] for code in done], axis=0),
@@ -258,21 +321,17 @@
                 preferred_element_type=F32,
             )
             for k, code in enumerate(done):
-                to_row = jnp.where(jnp.logical_or(turn < 2, ((code >> 22) & 1) == 1), HALF, code & 127)
+                to_row = jnp.where(jnp.logical_or(turn < 2, ((code >> 23) & 1) == 1), HALF, code & 127)
                 to_col = jnp.where(
-                    jnp.logical_or(turn < 2, ((code >> 21) & 1) == 1), COLS, (code >> 7) & 127
+                    jnp.logical_or(turn < 2, ((code >> 22) & 1) == 1), COLS, (code >> 7) & 127
                 )
                 own = (slice(k * VECS, (k + 1) * VECS), slice(k * BLK, (k + 1) * BLK))
                 sums.append((to_row, forward[own], to_col, backward[own]))
             for k in range(2):
                 slot = first + k
                 tiles[slot] = tile_values(waiting[slot, :, 0:BLK], waiting[slot, :, BLK:])
-                code = codes[opening + slot]
-                waiting[slot] = jnp.dot(
-                    features[(code >> 7) & 127][:, 0:DEPTH],
-                    pair_operand(code, row_data, steps),
-                    preferred_element_type=F32,
-                )
+                code = codes[0, opening + slot]
+                waiting[slot] = pair_products(code, operands, features, step_rows, step_lanes)
         for to_row, forward, to_col, backward in sums:
             row_acc[to_row] += forward
             col_acc[to_col] += backward
@@ -284,20 +343,35 @@
 def near_far_kernel(phase, *refs):
     place, counts, codes = refs[0:3]
     pieces = refs[3:7]
-    vectors, features, steps = refs[7:10]
-    col_in = refs[10:11] if phase == 1 else ()
-    outs = refs[10 + len(col_in) : -5]
-    row_data, row_acc, col_acc, waiting, tiles = refs[-5:]
+    vectors, features, step_rows, step_lanes = refs[7:11]
+    col_in = refs[11:12] if phase == 1 else ()
+    outs = refs[11 + len(col_in) : -6]
+    row_data, operands, row_acc, col_acc, waiting, tiles = refs[-6:]
     position = place[1] & 3
     for k, piece in enumerate(pieces):
         start = pl.multiple_of(((position - k) & 3) * BLOCKS, BLOCKS)
         row_data[pl.ds(start, BLOCKS)] = piece[...]
+    row_operands(row_data, operands)
     row_acc[...] = jnp.zeros_like(row_acc)
     if phase == 0:
         col_acc[...] = jnp.zeros_like(col_acc)
     else:
         col_acc[0:COLS] = col_in[0][...]
-    pair_loop(phase, counts, codes, row_data, vectors, features, steps, row_acc, col_acc, waiting, tiles)
+    pair_loop(
+        phase,
+        counts,
+        codes,
+        row_data,
+        operands,
+        vectors,
+        features,
+        step_rows,
+        step_lanes,
+        row_acc,
+        col_acc,
+        waiting,
+        tiles,
+    )
     for k in range(4):
         start = pl.multiple_of(((position + k) & 3) * BLOCKS, BLOCKS)
         outs[k][...] = row_acc[pl.ds(start, BLOCKS)].astype(outs[k].dtype)
@@ -368,12 +442,18 @@
 
 
 def step_tables():
-    level = lax.broadcasted_iota(jnp.int32, (17, 8, BLK), 1)
-    which = lax.broadcasted_iota(jnp.int32, (17, 8, BLK), 0)
-    along_x = jnp.where(level == 0, CELL[0] * which.astype(F32), jnp.where(level == 7, -1.0, 0.0))
-    along_y = jnp.where(level == 1, CELL[1] * (which - 7).astype(F32), 0.0)
-    along_z = jnp.where(level == 2, CELL[2] * (which - 14).astype(F32), 0.0)
-    return jnp.where(which < 3, along_x, jnp.where(which < 12, along_y, along_z))
+    x, y, z = np.meshgrid(np.arange(3), np.arange(-4, 5), np.arange(-2, 3), indexing="ij")
+    steps = np.stack([x, y, z], axis=-1).reshape(-1, 3) * np.array(CELL)
+    squared = np.sum(steps * steps, axis=1).astype(np.float32)
+    coarse = squared.astype(ml_dtypes.bfloat16).astype(np.float32)
+    rows = np.zeros((len(steps), 16, BLK), np.float32)
+    rows[:, 0:3] = rows[:, 3:6] = 2.0 * steps[:, :, None]
+    rows[:, 6] = coarse[:, None]
+    rows[:, 7] = (squared - coarse)[:, None]
+    rows[:, 8:11] = 1.0
+    lanes = np.zeros((len(steps), 16, BLK), np.float32)
+    lanes[:, :, 0:3] = lanes[:, :, 3:6] = -2.0 * steps[:, None, :]
+    return rows.astype(ml_dtypes.bfloat16), lanes.astype(ml_dtypes.bfloat16)
 
 
 def passed_down(value, steps):
@@ -404,29 +484,37 @@
     packed = call(
         prep_kernel,
         shape((BLOCKS, ROWS, BLK), BF16),
-        [SMEM, VMEM, VMEM, VMEM, VMEM],
+        [SMEM, ANY, ANY, ANY, ANY],
         VMEM,
         "prep",
-        scratch=[pltpu.VMEM((8, BLOCKS * BLK), F32)],
+        scratch=[
+            pltpu.VMEM((8, BLOCKS * BLK), F32),
+            pltpu.VMEM((3, BLOCKS * BLK), F32),
+            pltpu.VMEM((1, BLOCKS * BLK), jnp.int32),
+            pltpu.VMEM((VECS, BLOCKS * BLK), F32),
+            pltpu.VMEM((BLOCKS, BLK), jnp.int32),
+            pltpu.SemaphoreType.DMA((4,)),
+        ],
+        vmem=62,
     )(place, positions, kinds, krylov, order)
 
     other = across(packed)
     after = passed_down(packed, 1)
     second = passed_down(packed, 2)
-    rows_list, _ = lax.optimization_barrier((pair_rows.reshape(-1), packed))
+    rows_list, _ = lax.optimization_barrier((pair_rows.reshape(1, SLOTS), packed))
 
     inverse, codes, counts = call(
         side_kernel,
         (
             shape((BLOCKS, BLK), jnp.int32),
-            shape((2 * SLOT_SPAN + 1,), jnp.int32),
+            shape((1, 2 * SLOT_SPAN), jnp.int32),
             shape((2,), jnp.int32),
         ),
-        [SMEM, SMEM, SMEM, SMEM, VMEM],
-        (VMEM, SMEM, SMEM),
+        [SMEM, SMEM, VMEM, VMEM, VMEM],
+        (VMEM, VMEM, SMEM),
         "side",
         cost=time_cost(12),
-    )(place, rows_list, pair_cols.reshape(-1), pair_count.reshape(-1), order)
+    )(place, pair_count.reshape(-1), rows_list, pair_cols.reshape(1, SLOTS), order)
 
     near_rows = [packed] + [around(packed, k) for k in (1, 2, 3)]
 
@@ -440,9 +528,11 @@
     )(type_width, packed, after, second)
 
     far_rows = [other] + [around(other, k) for k in (1, 2, 3)]
-    steps, _ = lax.optimization_barrier((step_tables(), other))
+    step_rows, step_lanes = step_tables()
+    codes, _ = lax.optimization_barrier((codes, other))
     scratch = [
         pltpu.VMEM((HALF, ROWS, BLK), BF16),
+        pltpu.VMEM((HALF, 64, BLK), BF16),
         pltpu.VMEM((HALF + 1, VECS, BLK), F32),
         pltpu.VMEM((COLS + 1, VECS, BLK), F32),
         pltpu.VMEM((UNROLL, BLK, 2 * BLK), F32),
@@ -452,22 +542,22 @@
     *near_sums, col_sums = call(
         functools.partial(near_far_kernel, 0),
         [shape(block_set, F32)] + [shape(block_set, BF16)] * 3 + [shape((COLS, VECS, BLK), F32)],
-        [SMEM] * 3 + [VMEM] * 7,
+        [SMEM] * 3 + [VMEM] * 8,
         [VMEM] * 5,
         "pairs_near",
         scratch=scratch,
         cost=PAIR_COST,
-    )(place, counts, codes, *near_rows, vectors, features, steps)
+    )(place, counts, codes, *near_rows, vectors, features, step_rows, step_lanes)
 
     *far_sums, own_sum, after_sum, last_sum = call(
         functools.partial(near_far_kernel, 1),
         [shape(block_set, BF16)] * 4 + [shape(block_set, F32)] + [shape(block_set, BF16)] * 2,
-        [SMEM] * 3 + [VMEM] * 8,
+        [SMEM] * 3 + [VMEM] * 9,
         [VMEM] * 7,
         "pairs_far",
         scratch=scratch,
         cost=PAIR_COST,
-    )(place, counts, codes, *far_rows, vectors, features, steps, col_sums)
+    )(place, counts, codes, *far_rows, vectors, features, step_rows, step_lanes, col_sums)
 
     far_parts = [far_sums[0]] + [around(far_sums[k], k) for k in (1, 2, 3)]
     from_prior = passed_up(after_sum, 1)

time: 110 us -> 107 us (0.973)
  the two profiles are of different devices: /device:TPU:5 before, /device:TPU:6 now
where the time goes in v2:
time: 107 us; the launch traced here: 108 us
  starting transfers between devices  48.4 us (45%)
  Pallas kernels  42.5 us (40%)
  waiting for transfers between devices  11.4 us (11%)
  local copies, waits for them, and re-layouts  4.35 us (4%)
    ppermute x2, starting transfers between devices, passed_up(): lax.ppermute(value, 'row', [(s, s + steps) for s in range(count - steps)])  21.2 us
    pallas_call x1, Pallas kernels, on_device(): call(functools.partial(near_far_kernel, 0), [shape(block_set, F32)] + [sh...  18.1 us
    ppermute x12, starting transfers between devices, around(): lax.ppermute(value, 'col', [(c, (c & 4) + (c + steps) % 4) for c in range...  15.4 us
    pallas_call x1, Pallas kernels, on_device(): call(functools.partial(near_far_kernel, 1), [shape(block_set, BF16)] * 4...  8.07 us
    ppermute x2, starting transfers between devices, across(): return lax.ppermute(value, 'col', [(c, c ^ 4) for c in range(8)])  7.28 us
    ppermute x12, waiting for transfers between devices, around(): lax.ppermute(value, 'col', [(c, (c & 4) + (c + steps) % 4) for c in range...  6.93 us
    pallas_call x1, Pallas kernels, on_device(): call(prep_kernel, shape((BLOCKS, ROWS, BLK), BF16), [SMEM, ANY, ANY, ANY,...  6.92 us
    ppermute x2, starting transfers between devices, passed_down(): lax.ppermute(value, 'row', [(s, s - steps) for s in range(steps, count)])  4.64 us
  transfers between devices with their start and end apart: 18, of which 3 were waited for; matrix products, arithmetic and copies ran while one was open for 0% of the time, Pallas kernels for 22%

profile of v2, /device:TPU:6, one launch (start us, length us, event | category | flops | bytes accessed | tf_op | source)
XLA Modules:
  0.0 108.2 jit_solution(17804754579688458072)
XLA Ops:
  0.0 0.6 pad_add_fusion.place.refs_0_
  0.6 6.9 %prep.1.own.refs_3_ = bf16[32,24,128]{2,1,0:T(8,128)(2,1)} custom-call(s32[2]{0:T(128)} %pad_add_fusion.place.refs_0_, f32[3,4096]{1,0:T(4,128)} %positions_hbm.1, s32[1,4096]{1,0:T(1,128)} %bitcast.8, f32[16,4096]{1,0:T(8,128)} %refs_9_.3, s32[32,128]{1,0:T(8,128)} %bitcast.10), custom_call_target="tpu_custom_call" | custom-call | tf_op jit(solution)/shard_map/prep/pallas_call | solution.py:484
  7.5 3.1 %collective-permute-start.8 = (bf16[32,24,128]{2,1,0:T(8,128)(2,1)}, bf16[32,24,128]{2,1,0:T(8,128)(2,1)S(1)}, u32[]{:S(2)}, u32[]{:S(2)}) collective-permute-start(bf16[32,24,128]{2,1,0:T(8,128)(2,1)} %prep.1.own.refs_3_), channel_id=1, source_target_pairs={{0,3},{1,0},{2,1},{3,2},{4,7},{5,4},{6,5},{7,6},{8,11},{9,8},{10,9... | collective-permute-start | bytes 589832 | tf_op jit(solution)/shard_map/ppermute | solution.py:474
  10.6 0.6 collective-permute-start.7
  11.2 2.7 %collective-permute-start.5 = (bf16[32,24,128]{2,1,0:T(8,128)(2,1)}, bf16[32,24,128]{2,1,0:T(8,128)(2,1)S(1)}, u32[]{:S(2)}, u32[]{:S(2)}) collective-permute-start(bf16[32,24,128]{2,1,0:T(8,128)(2,1)} %prep.1.own.refs_3_), channel_id=1, source_target_pairs={{16,0},{24,8},{32,16},{40,24},{48,32},{56,40},{64,48},{72,56},{80,... | collective-permute-start | bytes 589832 | tf_op jit(solution)/shard_map/ppermute | solution.py:461
  14.0 1.9 %collective-permute-start.4 = (bf16[32,24,128]{2,1,0:T(8,128)(2,1)}, bf16[32,24,128]{2,1,0:T(8,128)(2,1)S(1)}, u32[]{:S(2)}, u32[]{:S(2)}) collective-permute-start(bf16[32,24,128]{2,1,0:T(8,128)(2,1)} %prep.1.own.refs_3_), channel_id=1, source_target_pairs={{8,0},{16,8},{24,16},{32,24},{40,32},{48,40},{56,48},{64,56},{72,6... | collective-permute-start | bytes 589832 | tf_op jit(solution)/shard_map/ppermute | solution.py:461
  15.9 7.3 %collective-permute-start = (bf16[32,24,128]{2,1,0:T(8,128)(2,1)}, bf16[32,24,128]{2,1,0:T(8,128)(2,1)S(1)}, u32[]{:S(2)}, u32[]{:S(2)}) collective-permute-start(bf16[32,24,128]{2,1,0:T(8,128)(2,1)} %prep.1.own.refs_3_), channel_id=1, source_target_pairs={{0,4},{1,5},{2,6},{3,7},{4,0},{5,1},{6,2},{7,3},{8,12},{9,13},{10,... | collective-permute-start | bytes 589832 | tf_op jit(solution)/shard_map/ppermute | solution.py:470
  23.8 0.7 copy-done.3
  24.6 0.6 copy-done.4
  25.2 0.7 copy-done.7
  25.8 0.7 copy-done.8
  26.5 1.8 %side.1 = (s32[32,128]{1,0:T(8,128)S(1)}, s32[1,1280]{1,0:T(1,128)S(1)}, s32[2]{0:T(128)S(1)}) custom-call(s32[2]{0:T(128)S(1)} %copy-done.4, s32[1]{0:T(128)} %bitcast.7.count, s32[1,512]{1,0:T(1,128)S(1)} %bitcast.12, s32[1,512]{1,0:T(1,128)S(1)} %bitcast.13, s32[32,128]{1,0:T(8,128)S(1)} %bitcast.11), custom_call_target="tpu_custom_call" | custom-call | flops 12000000000 | bytes 1000000 | tf_op jit(solution)/shard_map/side/pallas_call | solution.py:506
  28.4 0.0 copy-start.10
  28.4 1.0 collective-permute-start.6
  29.5 2.3 %collective-permute-start.3 = (bf16[32,24,128]{2,1,0:T(8,128)(2,1)S(1)}, bf16[32,24,128]{2,1,0:T(8,128)(2,1)S(1)}, u32[]{:S(2)}, u32[]{:S(2)}) collective-permute-start(bf16[32,24,128]{2,1,0:T(8,128)(2,1)S(1)} %collective-permute-done.refs_3_), channel_id=1, source_target_pairs={{0,3},{1,0},{2,1},{3,2},{4,7},{5,4},{6,5},{7,6},{8,11},{9,8},{10,9... | collective-permute-start | bytes 589832 | tf_op jit(solution)/shard_map/ppermute | solution.py:474
  31.7 1.7 %collective-permute-start.2 = (bf16[32,24,128]{2,1,0:T(8,128)(2,1)S(1)}, bf16[32,24,128]{2,1,0:T(8,128)(2,1)S(1)}, u32[]{:S(2)}, u32[]{:S(2)}) collective-permute-start(bf16[32,24,128]{2,1,0:T(8,128)(2,1)S(1)} %collective-permute-done.refs_3_), channel_id=1, source_target_pairs={{0,2},{1,3},{2,0},{3,1},{4,6},{5,7},{6,4},{7,5},{8,10},{9,11},{10,... | collective-permute-start | bytes 589832 | tf_op jit(solution)/shard_map/ppermute | solution.py:474
  33.4 3.6 %features.1 = (bf16[96,128,128]{2,1,0:T(8,128)(2,1)S(1)}, bf16[96,16,128]{2,1,0:T(8,128)(2,1)S(1)}) custom-call(f32[6]{0:T(128)S(1)} %copy-done.9, bf16[32,24,128]{2,1,0:T(8,128)(2,1)S(1)} %copy-done.1, bf16[32,24,128]{2,1,0:T(8,128)(2,1)S(1)} %collective-permute-done.4.after, bf16[32,24,128]{2,1,0:T(8,128)(2,1)S(1)} %collective-permute-done.5.second), custom_call_target="tpu_custom_call" | custom-call | flops 5000000000 | bytes 1000000 | tf_op jit(solution)/shard_map/features/pallas_call | solution.py:521
  37.1 1.6 %copy-done.12 = bf16[96,128,128]{2,1,0:T(8,128)(2,1)} copy-done((bf16[96,128,128]{2,1,0:T(8,128)(2,1)}, bf16[96,128,128]{2,1,0:T(8,128)(2,1)S(1)}, u32[]{:S(2)}) %copy-start.12) | copy-done | bytes 3145752
  38.8 18.1 %pairs_near.1 = (f32[32,16,128]{2,1,0:T(8,128)S(1)}, bf16[32,16,128]{2,1,0:T(8,128)(2,1)S(1)}, bf16[32,16,128]{2,1,0:T(8,128)(2,1)S(1)}, bf16[32,16,128]{2,1,0:T(8,128)(2,1)S(1)}, f32[96,16,128]{2,1,0:T(8,128)S(1)}) custom-call(s32[2]{0:T(128)S(1)} %copy-done.5, s32[2]{0:T(128)S(1)} %get-tuple-element.29.refs_1_, s32[1,1280]{1,0:T(1,128)S(1)} %get-tuple-element.31.refs_2_, ...), custom_call_target="tpu_custom_call" | custom-call | flops 16000000000 | bytes 1000000 | tf_op jit(solution)/shard_map/pairs_near/pallas_call | solution.py:542
  56.9 8.1 %pairs_far.1 = (bf16[32,16,128]{2,1,0:T(8,128)(2,1)S(1)}, bf16[32,16,128]{2,1,0:T(8,128)(2,1)S(1)}, bf16[32,16,128]{2,1,0:T(8,128)(2,1)S(1)}, bf16[32,16,128]{2,...) custom-call(s32[2]{0:T(128)S(1)} %copy-done.5, ...), custom_call_target="tpu_custom_call" | custom-call | flops 16000000000 | bytes 1000000 | tf_op jit(solution)/shard_map/pairs_far/pallas_call | solution.py:552
  65.0 0.3 collective-permute-start.11
  65.2 3.1 %collective-permute-start.13 = (bf16[32,16,128]{2,1,0:T(8,128)(2,1)S(1)}, bf16[32,16,128]{2,1,0:T(8,128)(2,1)S(1)}, u32[]{:S(2)}, u32[]{:S(2)}) collective-permute-start(bf16[32,16,128]{2,1,0:T(8,128)(2,1)S(1)} %get-tuple-element.45), channel_id=1, source_target_pairs={{0,3},{1,0},{2,1},{3,2},{4,7},{5,4},{6,5},{7,6},{8,11},{9,8},{10,9... | collective-permute-start | bytes 393224 | tf_op jit(solution)/shard_map/ppermute | solution.py:474
  68.3 7.9 %collective-permute-start.9 = (bf16[32,16,128]{2,1,0:T(8,128)(2,1)S(1)}, bf16[32,16,128]{2,1,0:T(8,128)(2,1)S(1)}, u32[]{:S(2)}, u32[]{:S(2)}) collective-permute-start(bf16[32,16,128]{2,1,0:T(8,128)(2,1)S(1)} %get-tuple-element.36), channel_id=1, source_target_pairs={{0,8},{8,16},{16,24},{24,32},{32,40},{40,48},{48,56},{56,64},{64,7... | collective-permute-start | bytes 393224 | tf_op jit(solution)/shard_map/ppermute | solution.py:466
  76.2 13.2 %collective-permute-start.10 = (bf16[32,16,128]{2,1,0:T(8,128)(2,1)S(1)}, bf16[32,16,128]{2,1,0:T(8,128)(2,1)S(1)}, u32[]{:S(2)}, u32[]{:S(2)}) collective-permute-start(bf16[32,16,128]{2,1,0:T(8,128)(2,1)S(1)} %get-tuple-element.37), channel_id=1, source_target_pairs={{0,16},{8,24},{16,32},{24,40},{32,48},{40,56},{48,64},{56,72},{64,... | collective-permute-start | bytes 393224 | tf_op jit(solution)/shard_map/ppermute | solution.py:466
  89.5 0.1 far_sum.1
  89.6 0.1 collective-permute-start.14
  89.6 1.5 %collective-permute-start.15 = (bf16[32,16,128]{2,1,0:T(8,128)(2,1)S(1)}, bf16[32,16,128]{2,1,0:T(8,128)(2,1)S(1)}, u32[]{:S(2)}, u32[]{:S(2)}) collective-permute-start(bf16[32,16,128]{2,1,0:T(8,128)(2,1)S(1)} %get-tuple-element.48), channel_id=1, source_target_pairs={{0,2},{1,3},{2,0},{3,1},{4,6},{5,7},{6,4},{7,5},{8,10},{9,11},{10,... | collective-permute-start | bytes 393224 | tf_op jit(solution)/shard_map/ppermute | solution.py:474
  91.1 1.8 %collective-permute-start.16 = (bf16[32,16,128]{2,1,0:T(8,128)(2,1)S(1)}, bf16[32,16,128]{2,1,0:T(8,128)(2,1)S(1)}, u32[]{:S(2)}, u32[]{:S(2)}) collective-permute-start(bf16[32,16,128]{2,1,0:T(8,128)(2,1)S(1)} %get-tuple-element.49), channel_id=1, source_target_pairs={{0,3},{1,0},{2,1},{3,2},{4,7},{5,4},{6,5},{7,6},{8,11},{9,8},{10,9... | collective-permute-start | bytes 393224 | tf_op jit(solution)/shard_map/ppermute | solution.py:474
  92.9 6.3 %collective-permute-done.14.refs_4_ = bf16[32,16,128]{2,1,0:T(8,128)(2,1)S(1)} collective-permute-done((bf16[32,16,128]{2,1,0:T(8,128)(2,1)S(1)}, bf16[32,16,128]{2,1,0:T(8,128)(2,1)S(1)}, u32[]{:S(2)}, u32[]{:S(2)}) %collective-permute-start.14) | collective-permute-done | bytes 131104 | tf_op jit(solution)/shard_map/ppermute | solution.py:474
  99.2 0.6 collective-permute-done.16.refs_6_
  99.8 4.5 %collective-permute-done.17.refs_7_ = bf16[32,16,128]{2,1,0:T(8,128)(2,1)S(1)} collective-permute-done((bf16[32,16,128]{2,1,0:T(8,128)(2,1)S(1)}, bf16[32,16,128]{2,1,0:T(8,128)(2,1)S(1)}, u32[]{:S(2)}, u32[]{:S(2)}) %collective-permute-start.17) | collective-permute-done | bytes 131104 | tf_op jit(solution)/shard_map/ppermute | solution.py:470
  104.3 3.9 %final.1 = f32[16,4096]{1,0:T(8,128)} custom-call(f32[6]{0:T(128)S(1)} %copy-done.6, f32[32,16,128]{2,1,0:T(8,128)S(1)} %get-tuple-element.35.refs_0_, bf16[32,16,128]{2,1,0:T(8,128)(2,1)S(1)} %collective-permute-done.9.refs_1_, bf16[32,16,128]{2,1,0:T(8,128)(2,1)S(1)} %collective-permute-done.10.refs_2_, f32[32,16,128]{2,1,0:T(8,128)S(1)} %get-tuple-element.46.refs_3_, ...), custom_call_target="tpu_custom_call" | custom-call | tf_op jit(solution)/shard_map/final/pallas_call | solution.py:573
  (38 shorter events, 0.1 us)
Async XLA Ops:
  7.5 31.2 %collective-permute-start.8 = (bf16[32,24,128]{2,1,0:T(8,128)(2,1)}, bf16[32,24,128]{2,1,0:T(8,128)(2,1)S(1)}, u32[]{:S(2)}, u32[]{:S(2)}) collective-permute-start(bf16[32,24,128]{2,1,0:T(8,128)(2,1)} %prep.1.own.refs_3_), channel_id=1, source_target_pairs={{0,3},{1,0},{2,1},{3,2},{4,7},{5,4},{6,5},{7,6},{8,11},{9,8},{10,9... | collective-permute-start | bytes 589832 | tf_op jit(solution)/shard_map/ppermute | solution.py:474
  10.6 28.1 %collective-permute-start.7 = (bf16[32,24,128]{2,1,0:T(8,128)(2,1)}, bf16[32,24,128]{2,1,0:T(8,128)(2,1)S(1)}, u32[]{:S(2)}, u32[]{:S(2)}) collective-permute-start(bf16[32,24,128]{2,1,0:T(8,128)(2,1)} %prep.1.own.refs_3_), channel_id=1, source_target_pairs={{0,2},{1,3},{2,0},{3,1},{4,6},{5,7},{6,4},{7,5},{8,10},{9,11},{10,... | collective-permute-start | bytes 589832 | tf_op jit(solution)/shard_map/ppermute | solution.py:474
  11.2 17.2 %collective-permute-start.5 = (bf16[32,24,128]{2,1,0:T(8,128)(2,1)}, bf16[32,24,128]{2,1,0:T(8,128)(2,1)S(1)}, u32[]{:S(2)}, u32[]{:S(2)}) collective-permute-start(bf16[32,24,128]{2,1,0:T(8,128)(2,1)} %prep.1.own.refs_3_), channel_id=1, source_target_pairs={{16,0},{24,8},{32,16},{40,24},{48,32},{56,40},{64,48},{72,56},{80,... | collective-permute-start | bytes 589832 | tf_op jit(solution)/shard_map/ppermute | solution.py:461
  14.0 17.8 %collective-permute-start.4 = (bf16[32,24,128]{2,1,0:T(8,128)(2,1)}, bf16[32,24,128]{2,1,0:T(8,128)(2,1)S(1)}, u32[]{:S(2)}, u32[]{:S(2)}) collective-permute-start(bf16[32,24,128]{2,1,0:T(8,128)(2,1)} %prep.1.own.refs_3_), channel_id=1, source_target_pairs={{8,0},{16,8},{24,16},{32,24},{40,32},{48,40},{56,48},{64,56},{72,6... | collective-permute-start | bytes 589832 | tf_op jit(solution)/shard_map/ppermute | solution.py:461
  15.9 13.6 %collective-permute-start = (bf16[32,24,128]{2,1,0:T(8,128)(2,1)}, bf16[32,24,128]{2,1,0:T(8,128)(2,1)S(1)}, u32[]{:S(2)}, u32[]{:S(2)}) collective-permute-start(bf16[32,24,128]{2,1,0:T(8,128)(2,1)} %prep.1.own.refs_3_), channel_id=1, source_target_pairs={{0,4},{1,5},{2,6},{3,7},{4,0},{5,1},{6,2},{7,3},{8,12},{9,13},{10,... | collective-permute-start | bytes 589832 | tf_op jit(solution)/shard_map/ppermute | solution.py:470
  23.8 0.7 copy-start.3
  24.5 0.6 copy-start.4
  25.2 0.7 copy-start.7
  25.8 0.7 copy-start.8
  26.5 1.9 %copy-start.1 = (bf16[32,24,128]{2,1,0:T(8,128)(2,1)S(1)}, bf16[32,24,128]{2,1,0:T(8,128)(2,1)}, u32[]{:S(2)}) copy-start(bf16[32,24,128]{2,1,0:T(8,128)(2,1)} %prep.1.own.refs_3_) | copy-start | bytes 589828
  26.5 6.9 %copy-start.9 = (f32[6]{0:T(128)S(1)}, f32[6]{0:T(128)}, u32[]{:S(2)}) copy-start(f32[6]{0:T(128)} %type_width.1) | copy-start | bytes 76
  28.4 10.4 %copy-start.5 = (s32[2]{0:T(128)S(1)}, s32[2]{0:T(128)}, u32[]{:S(2)}) copy-start(s32[2]{0:T(128)} %pad_add_fusion.place.refs_0_) | copy-start | bytes 28
  28.4 10.4 %copy-start.10 = (bf16[135,16,128]{2,1,0:T(8,128)(2,1)S(1)}, bf16[135,16,128]{2,1,0:T(8,128)(2,1)}, u32[]{:S(2)}) copy-start(bf16[135,16,128]{2,1,0:T(8,128)(2,1)} %constant.14.clone.refs_10_) | copy-start | bytes 1658884
  28.4 10.4 %copy-start.11 = (bf16[135,16,128]{2,1,0:T(8,128)(2,1)S(1)}, bf16[135,16,128]{2,1,0:T(8,128)(2,1)}, u32[]{:S(2)}) copy-start(bf16[135,16,128]{2,1,0:T(8,128)(2,1)} %constant.13.clone.refs_9_) | copy-start | bytes 1658884
  28.4 10.3 %collective-permute-start.6 = (bf16[32,24,128]{2,1,0:T(8,128)(2,1)S(1)}, bf16[32,24,128]{2,1,0:T(8,128)(2,1)S(1)}, u32[]{:S(2)}, u32[]{:S(2)}) collective-permute-start(bf16[32,24,128]{2,1,0:T(8,128)(2,1)S(1)} %copy-done.1), channel_id=1, source_target_pairs={{0,1},{1,2},{2,3},{3,0},{4,5},{5,6},{6,7},{7,4},{8,9},{9,10},{10,1... | collective-permute-start | bytes 589832 | tf_op jit(solution)/shard_map/ppermute | solution.py:474
  29.5 27.4 %collective-permute-start.3 = (bf16[32,24,128]{2,1,0:T(8,128)(2,1)S(1)}, bf16[32,24,128]{2,1,0:T(8,128)(2,1)S(1)}, u32[]{:S(2)}, u32[]{:S(2)}) collective-permute-start(bf16[32,24,128]{2,1,0:T(8,128)(2,1)S(1)} %collective-permute-done.refs_3_), channel_id=1, source_target_pairs={{0,3},{1,0},{2,1},{3,2},{4,7},{5,4},{6,5},{7,6},{8,11},{9,8},{10,9... | collective-permute-start | bytes 589832 | tf_op jit(solution)/shard_map/ppermute | solution.py:474
  31.7 25.1 %collective-permute-start.2 = (bf16[32,24,128]{2,1,0:T(8,128)(2,1)S(1)}, bf16[32,24,128]{2,1,0:T(8,128)(2,1)S(1)}, u32[]{:S(2)}, u32[]{:S(2)}) collective-permute-start(bf16[32,24,128]{2,1,0:T(8,128)(2,1)S(1)} %collective-permute-done.refs_3_), channel_id=1, source_target_pairs={{0,2},{1,3},{2,0},{3,1},{4,6},{5,7},{6,4},{7,5},{8,10},{9,11},{10,... | collective-permute-start | bytes 589832 | tf_op jit(solution)/shard_map/ppermute | solution.py:474
  37.1 1.6 %copy-start.12 = (bf16[96,128,128]{2,1,0:T(8,128)(2,1)}, bf16[96,128,128]{2,1,0:T(8,128)(2,1)S(1)}, u32[]{:S(2)}) copy-start(bf16[96,128,128]{2,1,0:T(8,128)(2,1)S(1)} %get-tuple-element.33.refs_8_) | copy-start | bytes 9437188
  38.7 18.1 %collective-permute-start.1 = (bf16[32,24,128]{2,1,0:T(8,128)(2,1)S(1)}, bf16[32,24,128]{2,1,0:T(8,128)(2,1)S(1)}, u32[]{:S(2)}, u32[]{:S(2)}) collective-permute-start(bf16[32,24,128]{2,1,0:T(8,128)(2,1)S(1)} %collective-permute-done.refs_3_), channel_id=1, source_target_pairs={{0,1},{1,2},{2,3},{3,0},{4,5},{5,6},{6,7},{7,4},{8,9},{9,10},{10,1... | collective-permute-start | bytes 589832 | tf_op jit(solution)/shard_map/ppermute | solution.py:474
  56.8 47.4 %copy-start = (f32[16,4096]{1,0:T(8,128)S(1)}, f32[16,4096]{1,0:T(8,128)}, u32[]{:S(2)}) copy-start(f32[16,4096]{1,0:T(8,128)} %refs_9_.3) | copy-start | bytes 786436
  56.9 47.4 %copy-start.2 = (s32[4096]{0:T(1024)S(1)}, s32[4096]{0:T(1024)}, u32[]{:S(2)}) copy-start(s32[4096]{0:T(1024)} %param.12) | copy-start | bytes 49156
  56.9 47.4 %copy-start.6 = (f32[6]{0:T(128)S(1)}, f32[6]{0:T(128)}, u32[]{:S(2)}) copy-start(f32[6]{0:T(128)} %type_hard.1) | copy-start | bytes 76
  65.0 24.5 %collective-permute-start.11 = (bf16[32,16,128]{2,1,0:T(8,128)(2,1)S(1)}, bf16[32,16,128]{2,1,0:T(8,128)(2,1)S(1)}, u32[]{:S(2)}, u32[]{:S(2)}) collective-permute-start(bf16[32,16,128]{2,1,0:T(8,128)(2,1)S(1)} %get-tuple-element.43), channel_id=1, source_target_pairs={{0,1},{1,2},{2,3},{3,0},{4,5},{5,6},{6,7},{7,4},{8,9},{9,10},{10,1... | collective-permute-start | bytes 393224 | tf_op jit(solution)/shard_map/ppermute | solution.py:474
  65.2 24.2 %collective-permute-start.12 = (bf16[32,16,128]{2,1,0:T(8,128)(2,1)S(1)}, bf16[32,16,128]{2,1,0:T(8,128)(2,1)S(1)}, u32[]{:S(2)}, u32[]{:S(2)}) collective-permute-start(bf16[32,16,128]{2,1,0:T(8,128)(2,1)S(1)} %get-tuple-element.44), channel_id=1, source_target_pairs={{0,2},{1,3},{2,0},{3,1},{4,6},{5,7},{6,4},{7,5},{8,10},{9,11},{10,... | collective-permute-start | bytes 393224 | tf_op jit(solution)/shard_map/ppermute | solution.py:474
  65.2 24.2 %collective-permute-start.13 = (bf16[32,16,128]{2,1,0:T(8,128)(2,1)S(1)}, bf16[32,16,128]{2,1,0:T(8,128)(2,1)S(1)}, u32[]{:S(2)}, u32[]{:S(2)}) collective-permute-start(bf16[32,16,128]{2,1,0:T(8,128)(2,1)S(1)} %get-tuple-element.45), channel_id=1, source_target_pairs={{0,3},{1,0},{2,1},{3,2},{4,7},{5,4},{6,5},{7,6},{8,11},{9,8},{10,9... | collective-permute-start | bytes 393224 | tf_op jit(solution)/shard_map/ppermute | solution.py:474
  68.3 24.6 %collective-permute-start.9 = (bf16[32,16,128]{2,1,0:T(8,128)(2,1)S(1)}, bf16[32,16,128]{2,1,0:T(8,128)(2,1)S(1)}, u32[]{:S(2)}, u32[]{:S(2)}) collective-permute-start(bf16[32,16,128]{2,1,0:T(8,128)(2,1)S(1)} %get-tuple-element.36), channel_id=1, source_target_pairs={{0,8},{8,16},{16,24},{24,32},{32,40},{40,48},{48,56},{56,64},{64,7... | collective-permute-start | bytes 393224 | tf_op jit(solution)/shard_map/ppermute | solution.py:466
  76.2 16.7 %collective-permute-start.10 = (bf16[32,16,128]{2,1,0:T(8,128)(2,1)S(1)}, bf16[32,16,128]{2,1,0:T(8,128)(2,1)S(1)}, u32[]{:S(2)}, u32[]{:S(2)}) collective-permute-start(bf16[32,16,128]{2,1,0:T(8,128)(2,1)S(1)} %get-tuple-element.37), channel_id=1, source_target_pairs={{0,16},{8,24},{16,32},{24,40},{32,48},{40,56},{48,64},{56,72},{64,... | collective-permute-start | bytes 393224 | tf_op jit(solution)/shard_map/ppermute | solution.py:466
  89.6 9.6 %collective-permute-start.14 = (bf16[32,16,128]{2,1,0:T(8,128)(2,1)S(1)}, bf16[32,16,128]{2,1,0:T(8,128)(2,1)S(1)}, u32[]{:S(2)}, u32[]{:S(2)}) collective-permute-start(bf16[32,16,128]{2,1,0:T(8,128)(2,1)S(1)} %get-tuple-element.47), channel_id=1, source_target_pairs={{0,1},{1,2},{2,3},{3,0},{4,5},{5,6},{6,7},{7,4},{8,9},{9,10},{10,1... | collective-permute-start | bytes 393224 | tf_op jit(solution)/shard_map/ppermute | solution.py:474
  89.6 9.5 %collective-permute-start.15 = (bf16[32,16,128]{2,1,0:T(8,128)(2,1)S(1)}, bf16[32,16,128]{2,1,0:T(8,128)(2,1)S(1)}, u32[]{:S(2)}, u32[]{:S(2)}) collective-permute-start(bf16[32,16,128]{2,1,0:T(8,128)(2,1)S(1)} %get-tuple-element.48), channel_id=1, source_target_pairs={{0,2},{1,3},{2,0},{3,1},{4,6},{5,7},{6,4},{7,5},{8,10},{9,11},{10,... | collective-permute-start | bytes 393224 | tf_op jit(solution)/shard_map/ppermute | solution.py:474
  91.1 8.7 %collective-permute-start.16 = (bf16[32,16,128]{2,1,0:T(8,128)(2,1)S(1)}, bf16[32,16,128]{2,1,0:T(8,128)(2,1)S(1)}, u32[]{:S(2)}, u32[]{:S(2)}) collective-permute-start(bf16[32,16,128]{2,1,0:T(8,128)(2,1)S(1)} %get-tuple-element.49), channel_id=1, source_target_pairs={{0,3},{1,0},{2,1},{3,2},{4,7},{5,4},{6,5},{7,6},{8,11},{9,8},{10,9... | collective-permute-start | bytes 393224 | tf_op jit(solution)/shard_map/ppermute | solution.py:474
  92.9 11.4 %collective-permute-start.17 = (bf16[32,16,128]{2,1,0:T(8,128)(2,1)S(1)}, bf16[32,16,128]{2,1,0:T(8,128)(2,1)S(1)}, u32[]{:S(2)}, u32[]{:S(2)}) collective-permute-start(bf16[32,16,128]{2,1,0:T(8,128)(2,1)S(1)} %far_sum.1), channel_id=1, source_target_pairs={{0,4},{1,5},{2,6},{3,7},{4,0},{5,1},{6,2},{7,3},{8,12},{9,13},{10,... | collective-permute-start | bytes 393224 | tf_op jit(solution)/shard_map/ppermute | solution.py:470

commit v3 on v2

--- a/solution.py
+++ b/solution.py
@@ -65,8 +65,12 @@
     return jnp.take_along_axis(source, index, axis=1, mode="promise_in_bounds")
 
 
+def here():
+    return lax.axis_index("row"), lax.axis_index("col")
+
+
 def prep_kernel(
-    place, positions_hbm, type_hbm, krylov_hbm, order_hbm, packed, geometry, positions, atom_type, krylov, order, done
+    positions_hbm, type_hbm, krylov_hbm, order_hbm, packed, geometry, positions, atom_type, krylov, order, done
 ):
     loads = [
         pltpu.make_async_copy(source, target, done.at[k])
@@ -81,9 +85,10 @@
     ]
     for load in loads:
         load.start()
+    place = here()
+    geometry[...] = jnp.zeros_like(geometry)
     for load in loads:
         load.wait()
-    geometry[...] = jnp.zeros_like(geometry)
     geometry[0:3, :] = positions[...]
     geometry[3:4, :] = atom_type[...].astype(F32)
     level = sublane()
@@ -118,7 +123,20 @@
     lax.fori_loop(0, BLOCKS, one_block, 0)
 
 
-def side_kernel(place, count, rows, cols, order, inverse, codes, counts):
+def side_kernel(
+    count_hbm, rows_hbm, cols_hbm, order_hbm, inverse, codes, counts, count, rows, cols, order, done
+):
+    loads = [
+        pltpu.make_async_copy(source, target, done.at[k])
+        for k, (source, target) in enumerate(
+            ((count_hbm, count), (rows_hbm, rows), (cols_hbm, cols), (order_hbm, order))
+        )
+    ]
+    for load in loads:
+        load.start()
+    place = here()
+    for load in loads:
+        load.wait()
     row = rows[...]
     col = cols[...] - place[0] * BLOCKS
     step_y = place[1] - (row >> 5) + 4
@@ -126,7 +144,7 @@
     step = ((col >> 5) * 9 + step_y) * 5 + step_z
     diagonal = jnp.logical_and(col < BLOCKS, row == place[1] * BLOCKS + col)
     code = (row & 127) | (col << 7) | (step << 14) | (diagonal.astype(jnp.int32) << 22)
-    live = lax.broadcasted_iota(jnp.int32, (1, SLOTS), 1) < count[0]
+    live = lax.broadcasted_iota(jnp.int32, (1, SLOTS), 1) < count[0, 0]
     same = (row >> 7) == (place[1] >> 2)
     near = jnp.logical_and(live, same).astype(F32)
     far = jnp.logical_and(live, jnp.logical_not(same)).astype(F32)
@@ -341,13 +359,13 @@
 
 
 def near_far_kernel(phase, *refs):
-    place, counts, codes = refs[0:3]
-    pieces = refs[3:7]
-    vectors, features, step_rows, step_lanes = refs[7:11]
-    col_in = refs[11:12] if phase == 1 else ()
-    outs = refs[11 + len(col_in) : -6]
+    counts, codes = refs[0:2]
+    pieces = refs[2:6]
+    vectors, features, step_rows, step_lanes = refs[6:10]
+    col_in = refs[10:11] if phase == 1 else ()
+    outs = refs[10 + len(col_in) : -6]
     row_data, operands, row_acc, col_acc, waiting, tiles = refs[-6:]
-    position = place[1] & 3
+    position = here()[1] & 3
     for k, piece in enumerate(pieces):
         start = pl.multiple_of(((position - k) & 3) * BLOCKS, BLOCKS)
         row_data[pl.ds(start, BLOCKS)] = piece[...]
@@ -428,7 +446,7 @@
     return jax.ShapeDtypeStruct(dims, dtype)
 
 
-def call(kernel, out_shape, in_specs, out_specs, name, scratch=(), vmem=48, cost=None):
+def call(kernel, out_shape, in_specs, out_specs, name, scratch=(), vmem=20, cost=None):
     return pl.pallas_call(
         kernel,
         out_shape=out_shape,
@@ -477,14 +495,13 @@
 def on_device(
     positions, atom_type, krylov, block_order, type_width, type_hard, pair_rows, pair_cols, pair_count
 ):
-    place = jnp.stack([lax.axis_index("row"), lax.axis_index("col")]).astype(jnp.int32)
     order = block_order.reshape(BLOCKS, BLK)
     kinds = atom_type.reshape(1, -1)
 
     packed = call(
         prep_kernel,
         shape((BLOCKS, ROWS, BLK), BF16),
-        [SMEM, ANY, ANY, ANY, ANY],
+        [ANY, ANY, ANY, ANY],
         VMEM,
         "prep",
         scratch=[
@@ -496,7 +513,7 @@
             pltpu.SemaphoreType.DMA((4,)),
         ],
         vmem=62,
-    )(place, positions, kinds, krylov, order)
+    )(positions, kinds, krylov, order)
 
     other = across(packed)
     after = passed_down(packed, 1)
@@ -510,12 +527,21 @@
             shape((1, 2 * SLOT_SPAN), jnp.int32),
             shape((2,), jnp.int32),
         ),
-        [SMEM, SMEM, VMEM, VMEM, VMEM],
+        [ANY, ANY, ANY, ANY],
         (VMEM, VMEM, SMEM),
         "side",
-        cost=time_cost(12),
-    )(place, pair_count.reshape(-1), rows_list, pair_cols.reshape(1, SLOTS), order)
-
+        scratch=[
+            pltpu.SMEM((1, 1), jnp.int32),
+            pltpu.VMEM((1, SLOTS), jnp.int32),
+            pltpu.VMEM((1, SLOTS), jnp.int32),
+            pltpu.VMEM((BLOCKS, BLK), jnp.int32),
+            pltpu.SemaphoreType.DMA((4,)),
+        ],
+        vmem=62,
+        cost=time_cost(2),
+    )(pair_count, rows_list, pair_cols.reshape(1, SLOTS), order)
+
+    codes, packed = lax.optimization_barrier((codes, packed))
     near_rows = [packed] + [around(packed, k) for k in (1, 2, 3)]
 
     features, vectors = call(
@@ -524,7 +550,7 @@
         [SMEM, VMEM, VMEM, VMEM],
         (VMEM, VMEM),
         "features",
-        cost=time_cost(5),
+        cost=time_cost(12),
     )(type_width, packed, after, second)
 
     far_rows = [other] + [around(other, k) for k in (1, 2, 3)]
@@ -542,22 +568,22 @@
     *near_sums, col_sums = call(
         functools.partial(near_far_kernel, 0),
         [shape(block_set, F32)] + [shape(block_set, BF16)] * 3 + [shape((COLS, VECS, BLK), F32)],
-        [SMEM] * 3 + [VMEM] * 8,
+        [SMEM] * 2 + [VMEM] * 8,
         [VMEM] * 5,
         "pairs_near",
         scratch=scratch,
         cost=PAIR_COST,
-    )(place, counts, codes, *near_rows, vectors, features, step_rows, step_lanes)
+    )(counts, codes, *near_rows, vectors, features, step_rows, step_lanes)
 
     *far_sums, own_sum, after_sum, last_sum = call(
         functools.partial(near_far_kernel, 1),
         [shape(block_set, BF16)] * 4 + [shape(block_set, F32)] + [shape(block_set, BF16)] * 2,
-        [SMEM] * 3 + [VMEM] * 9,
+        [SMEM] * 2 + [VMEM] * 9,
         [VMEM] * 7,
         "pairs_far",
         scratch=scratch,
         cost=PAIR_COST,
-    )(place, counts, codes, *far_rows, vectors, features, step_rows, step_lanes, col_sums)
+    )(counts, codes, *far_rows, vectors, features, step_rows, step_lanes, col_sums)
 
     far_parts = [far_sums[0]] + [around(far_sums[k], k) for k in (1, 2, 3)]
     from_prior = passed_up(after_sum, 1)
@@ -566,10 +592,10 @@
         sum_kernel, shape((BLOCKS, VECS, BLK), BF16), [VMEM] * 4, VMEM, "far_sum"
     )(*far_parts)
     from_far = across(far_sum)
-    near_sums, _ = lax.optimization_barrier((near_sums, far_sum))
+    near_sums, _ = lax.optimization_barrier((near_sums, (far_sum, from_prior, from_second)))
     near_parts = [near_sums[0]] + [around(near_sums[k], k) for k in (1, 2, 3)]
 
-    parts = [own_sum, from_prior, from_second, *near_parts, from_far]
+    parts = [own_sum, from_far, from_prior, from_second, *near_parts]
     return call(
         final_kernel,
         shape(krylov.shape, F32),

time: 107 us -> 99.4 us (0.929)
  the two profiles are of different devices: /device:TPU:6 before, /device:TPU:57 now
where the time goes in v3:
time: 99.4 us; the launch traced here: 99 us
  starting transfers between devices  48 us (48%)
  Pallas kernels  33.9 us (34%)
  waiting for transfers between devices  16.1 us (16%)
    ppermute x12, starting transfers between devices, around(): lax.ppermute(value, 'col', [(c, (c & 4) + (c + steps) % 4) for c in range...  27.4 us
    pallas_call x1, Pallas kernels, on_device(): call(functools.partial(near_far_kernel, 0), [shape(block_set, F32)] + [sh...  9.97 us
    pallas_call x1, Pallas kernels, on_device(): call(functools.partial(near_far_kernel, 1), [shape(block_set, BF16)] * 4...  7.6 us
    ppermute x2, starting transfers between devices, across(): return lax.ppermute(value, 'col', [(c, c ^ 4) for c in range(8)])  7.09 us
    ppermute x2, starting transfers between devices, passed_down(): lax.ppermute(value, 'row', [(s, s - steps) for s in range(steps, count)])  7.06 us
    ppermute x2, waiting for transfers between devices, passed_up(): lax.ppermute(value, 'row', [(s, s + steps) for s in range(count - steps)])  6.85 us
    ppermute x12, waiting for transfers between devices, around(): lax.ppermute(value, 'col', [(c, (c & 4) + (c + steps) % 4) for c in range...  6.43 us
    ppermute x2, starting transfers between devices, passed_up(): lax.ppermute(value, 'row', [(s, s + steps) for s in range(count - steps)])  6.42 us
  transfers between devices with their start and end apart: 18, of which 6 were waited for; matrix products, arithmetic and copies ran while one was open for 0% of the time, Pallas kernels for 16%

profile of v3, /device:TPU:57, one launch (start us, length us, event | category | flops | bytes accessed | tf_op | source)
XLA Modules:
  0.0 99.0 jit_solution(16972624010798298765)
XLA Ops:
  0.0 6.3 %prep.1.own.refs_2_ = bf16[32,24,128]{2,1,0:T(8,128)(2,1)} custom-call(f32[3,4096]{1,0:T(4,128)} %positions_hbm.1, s32[1,4096]{1,0:T(1,128)} %bitcast.4, f32[16,4096]{1,0:T(8,128)} %refs_9_.3, s32[32,128]{1,0:T(8,128)} %bitcast.6), custom_call_target="tpu_custom_call" | custom-call | tf_op jit(solution)/shard_map/prep/pallas_call | solution.py:501
  6.3 3.9 %collective-permute-start.5 = (bf16[32,24,128]{2,1,0:T(8,128)(2,1)}, bf16[32,24,128]{2,1,0:T(8,128)(2,1)S(1)}, u32[]{:S(2)}, u32[]{:S(2)}) collective-permute-start(bf16[32,24,128]{2,1,0:T(8,128)(2,1)} %prep.1.own.refs_2_), channel_id=1, source_target_pairs={{16,0},{24,8},{32,16},{40,24},{48,32},{56,40},{64,48},{72,56},{80,... | collective-permute-start | bytes 589832 | tf_op jit(solution)/shard_map/ppermute | solution.py:479
  10.2 7.0 %collective-permute-start = (bf16[32,24,128]{2,1,0:T(8,128)(2,1)}, bf16[32,24,128]{2,1,0:T(8,128)(2,1)S(1)}, u32[]{:S(2)}, u32[]{:S(2)}) collective-permute-start(bf16[32,24,128]{2,1,0:T(8,128)(2,1)} %prep.1.own.refs_2_), channel_id=1, source_target_pairs={{0,4},{1,5},{2,6},{3,7},{4,0},{5,1},{6,2},{7,3},{8,12},{9,13},{10,... | collective-permute-start | bytes 589832 | tf_op jit(solution)/shard_map/ppermute | solution.py:488
  17.2 3.1 %collective-permute-start.4 = (bf16[32,24,128]{2,1,0:T(8,128)(2,1)}, bf16[32,24,128]{2,1,0:T(8,128)(2,1)S(1)}, u32[]{:S(2)}, u32[]{:S(2)}) collective-permute-start(bf16[32,24,128]{2,1,0:T(8,128)(2,1)} %prep.1.own.refs_2_), channel_id=1, source_target_pairs={{8,0},{16,8},{24,16},{32,24},{40,32},{48,40},{56,48},{64,56},{72,6... | collective-permute-start | bytes 589832 | tf_op jit(solution)/shard_map/ppermute | solution.py:479
  21.0 0.0 copy-start.1
  21.0 2.5 %side.1 = (s32[32,128]{1,0:T(8,128)}, s32[1,1280]{1,0:T(1,128)}, s32[2]{0:T(128)}) custom-call(s32[1,1]{1,0:T(1,128)S(6)} %copy.12.count_hbm, s32[1,512]{1,0:T(1,128)} %bitcast.8, s32[1,512]{1,0:T(1,128)} %bitcast.9, s32[32,128]{1,0:T(8,128)} %bitcast.7), custom_call_target="tpu_custom_call" | custom-call | flops 2000000000 | bytes 1000000 | tf_op jit(solution)/shard_map/side/pallas_call | solution.py:523
  23.5 0.0 copy-start.6
  23.5 0.0 copy-start.7
  23.5 0.5 collective-permute-start.8
  24.1 0.7 collective-permute-start.7
  24.7 1.9 %collective-permute-start.6 = (bf16[32,24,128]{2,1,0:T(8,128)(2,1)S(1)}, bf16[32,24,128]{2,1,0:T(8,128)(2,1)S(1)}, u32[]{:S(2)}, u32[]{:S(2)}) collective-permute-start(bf16[32,24,128]{2,1,0:T(8,128)(2,1)S(1)} %copy-done.1), channel_id=1, source_target_pairs={{0,1},{1,2},{2,3},{3,0},{4,5},{5,6},{6,7},{7,4},{8,9},{9,10},{10,1... | collective-permute-start | bytes 589832 | tf_op jit(solution)/shard_map/ppermute | solution.py:492
  26.6 2.8 %collective-permute-done.refs_2_ = bf16[32,24,128]{2,1,0:T(8,128)(2,1)S(1)} collective-permute-done((bf16[32,24,128]{2,1,0:T(8,128)(2,1)}, bf16[32,24,128]{2,1,0:T(8,128)(2,1)S(1)}, u32[]{:S(2)}, u32[]{:S(2)}) %collective-permute-start) | collective-permute-done | bytes 196640 | tf_op jit(solution)/shard_map/ppermute | solution.py:488
  29.4 0.5 collective-permute-start.3
  29.9 0.7 collective-permute-start.2
  30.5 3.6 %features.1 = (bf16[96,128,128]{2,1,0:T(8,128)(2,1)S(1)}, bf16[96,16,128]{2,1,0:T(8,128)(2,1)S(1)}) custom-call(f32[6]{0:T(128)S(1)} %copy-done.5, bf16[32,24,128]{2,1,0:T(8,128)(2,1)S(1)} %copy-done.1, bf16[32,24,128]{2,1,0:T(8,128)(2,1)S(1)} %collective-permute-done.4.after, bf16[32,24,128]{2,1,0:T(8,128)(2,1)S(1)} %collective-permute-done.5.second), custom_call_target="tpu_custom_call" | custom-call | flops 12000000000 | bytes 1000000 | tf_op jit(solution)/shard_map/features/pallas_call | solution.py:547
  34.2 1.4 %collective-permute-done.8.refs_5_ = bf16[32,24,128]{2,1,0:T(8,128)(2,1)S(1)} collective-permute-done((bf16[32,24,128]{2,1,0:T(8,128)(2,1)S(1)}, bf16[32,24,128]{2,1,0:T(8,128)(2,1)S(1)}, u32[]{:S(2)}, u32[]{:S(2)}) %collective-permute-start.8) | collective-permute-done | bytes 196640 | tf_op jit(solution)/shard_map/ppermute | solution.py:492
  35.6 0.6 collective-permute-start.1
  36.2 10.0 %pairs_near.1 = (f32[32,16,128]{2,1,0:T(8,128)S(1)}, bf16[32,16,128]{2,1,0:T(8,128)(2,1)S(1)}, bf16[32,16,128]{2,1,0:T(8,128)(2,1)S(1)}, bf16[32,16,128]{2,1,0:T(8,128)(2,1)S(1)}, f32[96,16,128]{2,1,0:T(8,128)S(1)}) custom-call(s32[2]{0:T(128)S(1)} %copy-done.9, s32[1,1280]{1,0:T(1,128)S(1)} %copy-done.8, bf16[32,24,128]{2,1,0:T(8,128)(2,1)S(1)} %copy-done.1, ...), custom_call_target="tpu_custom_call" | custom-call | flops 16000000000 | bytes 1000000 | tf_op jit(solution)/shard_map/pairs_near/pallas_call | solution.py:568
  46.3 7.6 %pairs_far.1 = (bf16[32,16,128]{2,1,0:T(8,128)(2,1)S(1)}, bf16[32,16,128]{2,1,0:T(8,128)(2,1)S(1)}, bf16[32,16,128]{2,1,0:T(8,128)(2,1)S(1)}, bf16[32,16,128]{2,...) custom-call(s32[2]{0:T(128)S(1)} %copy-done.9, ...), custom_call_target="tpu_custom_call" | custom-call | flops 16000000000 | bytes 1000000 | tf_op jit(solution)/shard_map/pairs_far/pallas_call | solution.py:578
  53.9 15.3 %collective-permute-start.9 = (bf16[32,16,128]{2,1,0:T(8,128)(2,1)S(1)}, bf16[32,16,128]{2,1,0:T(8,128)(2,1)S(1)}, u32[]{:S(2)}, u32[]{:S(2)}) collective-permute-start(bf16[32,16,128]{2,1,0:T(8,128)(2,1)S(1)} %get-tuple-element.41), channel_id=1, source_target_pairs={{0,1},{1,2},{2,3},{3,0},{4,5},{5,6},{6,7},{7,4},{8,9},{9,10},{10,1... | collective-permute-start | bytes 393224 | tf_op jit(solution)/shard_map/ppermute | solution.py:492
  69.1 0.7 collective-permute-start.11
  69.8 4.5 %collective-permute-start.13 = (bf16[32,16,128]{2,1,0:T(8,128)(2,1)S(1)}, bf16[32,16,128]{2,1,0:T(8,128)(2,1)S(1)}, u32[]{:S(2)}, u32[]{:S(2)}) collective-permute-start(bf16[32,16,128]{2,1,0:T(8,128)(2,1)S(1)} %get-tuple-element.44), channel_id=1, source_target_pairs={{0,8},{8,16},{16,24},{24,32},{32,40},{40,48},{48,56},{56,64},{64,7... | collective-permute-start | bytes 393224 | tf_op jit(solution)/shard_map/ppermute | solution.py:484
  74.3 1.9 %collective-permute-start.14 = (bf16[32,16,128]{2,1,0:T(8,128)(2,1)S(1)}, bf16[32,16,128]{2,1,0:T(8,128)(2,1)S(1)}, u32[]{:S(2)}, u32[]{:S(2)}) collective-permute-start(bf16[32,16,128]{2,1,0:T(8,128)(2,1)S(1)} %get-tuple-element.45), channel_id=1, source_target_pairs={{0,16},{8,24},{16,32},{24,40},{32,48},{40,56},{48,64},{56,72},{64,... | collective-permute-start | bytes 393224 | tf_op jit(solution)/shard_map/ppermute | solution.py:484
  76.3 0.1 far_sum.1
  76.4 0.1 collective-permute-start.12
  76.5 6.9 %collective-permute-done.14.refs_3_ = bf16[32,16,128]{2,1,0:T(8,128)(2,1)S(1)} collective-permute-done((bf16[32,16,128]{2,1,0:T(8,128)(2,1)S(1)}, bf16[32,16,128]{2,1,0:T(8,128)(2,1)S(1)}, u32[]{:S(2)}, u32[]{:S(2)}) %collective-permute-start.14) | collective-permute-done | bytes 131104 | tf_op jit(solution)/shard_map/ppermute | solution.py:484
  83.3 2.0 %collective-permute-start.15 = (bf16[32,16,128]{2,1,0:T(8,128)(2,1)S(1)}, bf16[32,16,128]{2,1,0:T(8,128)(2,1)S(1)}, u32[]{:S(2)}, u32[]{:S(2)}) collective-permute-start(bf16[32,16,128]{2,1,0:T(8,128)(2,1)S(1)} %get-tuple-element.51), channel_id=1, source_target_pairs={{0,1},{1,2},{2,3},{3,0},{4,5},{5,6},{6,7},{7,4},{8,9},{9,10},{10,1... | collective-permute-start | bytes 393224 | tf_op jit(solution)/shard_map/ppermute | solution.py:492
  85.3 4.6 %collective-permute-start.16 = (bf16[32,16,128]{2,1,0:T(8,128)(2,1)S(1)}, bf16[32,16,128]{2,1,0:T(8,128)(2,1)S(1)}, u32[]{:S(2)}, u32[]{:S(2)}) collective-permute-start(bf16[32,16,128]{2,1,0:T(8,128)(2,1)S(1)} %get-tuple-element.52), channel_id=1, source_target_pairs={{0,2},{1,3},{2,0},{3,1},{4,6},{5,7},{6,4},{7,5},{8,10},{9,11},{10,... | collective-permute-start | bytes 393224 | tf_op jit(solution)/shard_map/ppermute | solution.py:492
  90.0 0.9 collective-permute-done.15.refs_5_
  90.8 1.6 %collective-permute-done.16.refs_6_ = bf16[32,16,128]{2,1,0:T(8,128)(2,1)S(1)} collective-permute-done((bf16[32,16,128]{2,1,0:T(8,128)(2,1)S(1)}, bf16[32,16,128]{2,1,0:T(8,128)(2,1)S(1)}, u32[]{:S(2)}, u32[]{:S(2)}) %collective-permute-start.16) | collective-permute-done | bytes 131104 | tf_op jit(solution)/shard_map/ppermute | solution.py:492
  92.4 2.6 %collective-permute-done.17.refs_7_ = bf16[32,16,128]{2,1,0:T(8,128)(2,1)S(1)} collective-permute-done((bf16[32,16,128]{2,1,0:T(8,128)(2,1)S(1)}, bf16[32,16,128]{2,1,0:T(8,128)(2,1)S(1)}, u32[]{:S(2)}, u32[]{:S(2)}) %collective-permute-start.17) | collective-permute-done | bytes 131104 | tf_op jit(solution)/shard_map/ppermute | solution.py:492
  95.0 3.9 %final.1 = f32[16,4096]{1,0:T(8,128)} custom-call(f32[6]{0:T(128)S(1)} %copy-done.4, f32[32,16,128]{2,1,0:T(8,128)S(1)} %get-tuple-element.39.refs_0_, bf16[32,16,128]{2,1,0:T(8,128)(2,1)S(1)} %collective-permute-done.12.refs_1_, bf16[32,16,128]{2,1,0:T(8,128)(2,1)S(1)} %collective-permute-done.13.refs_2_, ...), custom_call_target="tpu_custom_call" | custom-call | tf_op jit(solution)/shard_map/final/pallas_call | solution.py:599
  (31 shorter events, 0.1 us)
Async XLA Ops:
  6.3 18.5 %collective-permute-start.5 = (bf16[32,24,128]{2,1,0:T(8,128)(2,1)}, bf16[32,24,128]{2,1,0:T(8,128)(2,1)S(1)}, u32[]{:S(2)}, u32[]{:S(2)}) collective-permute-start(bf16[32,24,128]{2,1,0:T(8,128)(2,1)} %prep.1.own.refs_2_), channel_id=1, source_target_pairs={{16,0},{24,8},{32,16},{40,24},{48,32},{56,40},{64,48},{72,56},{80,... | collective-permute-start | bytes 589832 | tf_op jit(solution)/shard_map/ppermute | solution.py:479
  10.2 19.2 %collective-permute-start = (bf16[32,24,128]{2,1,0:T(8,128)(2,1)}, bf16[32,24,128]{2,1,0:T(8,128)(2,1)S(1)}, u32[]{:S(2)}, u32[]{:S(2)}) collective-permute-start(bf16[32,24,128]{2,1,0:T(8,128)(2,1)} %prep.1.own.refs_2_), channel_id=1, source_target_pairs={{0,4},{1,5},{2,6},{3,7},{4,0},{5,1},{6,2},{7,3},{8,12},{9,13},{10,... | collective-permute-start | bytes 589832 | tf_op jit(solution)/shard_map/ppermute | solution.py:488
  17.2 12.7 %collective-permute-start.4 = (bf16[32,24,128]{2,1,0:T(8,128)(2,1)}, bf16[32,24,128]{2,1,0:T(8,128)(2,1)S(1)}, u32[]{:S(2)}, u32[]{:S(2)}) collective-permute-start(bf16[32,24,128]{2,1,0:T(8,128)(2,1)} %prep.1.own.refs_2_), channel_id=1, source_target_pairs={{8,0},{16,8},{24,16},{32,24},{40,32},{48,40},{56,48},{64,56},{72,6... | collective-permute-start | bytes 589832 | tf_op jit(solution)/shard_map/ppermute | solution.py:479
  21.0 2.5 %copy-start.1 = (bf16[32,24,128]{2,1,0:T(8,128)(2,1)S(1)}, bf16[32,24,128]{2,1,0:T(8,128)(2,1)}, u32[]{:S(2)}) copy-start(bf16[32,24,128]{2,1,0:T(8,128)(2,1)} %prep.1.own.refs_2_) | copy-start | bytes 589828
  21.0 9.6 %copy-start.5 = (f32[6]{0:T(128)S(1)}, f32[6]{0:T(128)}, u32[]{:S(2)}) copy-start(f32[6]{0:T(128)} %type_width.1) | copy-start | bytes 76
  23.5 12.7 %copy-start.6 = (bf16[135,16,128]{2,1,0:T(8,128)(2,1)S(1)}, bf16[135,16,128]{2,1,0:T(8,128)(2,1)}, u32[]{:S(2)}) copy-start(bf16[135,16,128]{2,1,0:T(8,128)(2,1)} %constant.5.clone.refs_9_) | copy-start | bytes 1658884
  23.5 12.7 %copy-start.7 = (bf16[135,16,128]{2,1,0:T(8,128)(2,1)S(1)}, bf16[135,16,128]{2,1,0:T(8,128)(2,1)}, u32[]{:S(2)}) copy-start(bf16[135,16,128]{2,1,0:T(8,128)(2,1)} %constant.4.clone.refs_8_) | copy-start | bytes 1658884
  23.5 12.7 %copy-start.8 = (s32[1,1280]{1,0:T(1,128)S(1)}, s32[1,1280]{1,0:T(1,128)}, u32[]{:S(2)}) copy-start(s32[1,1280]{1,0:T(1,128)} %get-tuple-element.34.refs_1_) | copy-start | bytes 15364
  23.5 12.7 %copy-start.9 = (s32[2]{0:T(128)S(1)}, s32[2]{0:T(128)}, u32[]{:S(2)}) copy-start(s32[2]{0:T(128)} %get-tuple-element.31.refs_0_) | copy-start | bytes 28
  23.5 12.0 %collective-permute-start.8 = (bf16[32,24,128]{2,1,0:T(8,128)(2,1)S(1)}, bf16[32,24,128]{2,1,0:T(8,128)(2,1)S(1)}, u32[]{:S(2)}, u32[]{:S(2)}) collective-permute-start(bf16[32,24,128]{2,1,0:T(8,128)(2,1)S(1)} %copy-done.1), channel_id=1, source_target_pairs={{0,3},{1,0},{2,1},{3,2},{4,7},{5,4},{6,5},{7,6},{8,11},{9,8},{10,9... | collective-permute-start | bytes 589832 | tf_op jit(solution)/shard_map/ppermute | solution.py:492
  24.1 12.1 %collective-permute-start.7 = (bf16[32,24,128]{2,1,0:T(8,128)(2,1)S(1)}, bf16[32,24,128]{2,1,0:T(8,128)(2,1)S(1)}, u32[]{:S(2)}, u32[]{:S(2)}) collective-permute-start(bf16[32,24,128]{2,1,0:T(8,128)(2,1)S(1)} %copy-done.1), channel_id=1, source_target_pairs={{0,2},{1,3},{2,0},{3,1},{4,6},{5,7},{6,4},{7,5},{8,10},{9,11},{10,... | collective-permute-start | bytes 589832 | tf_op jit(solution)/shard_map/ppermute | solution.py:492
  24.7 11.4 %collective-permute-start.6 = (bf16[32,24,128]{2,1,0:T(8,128)(2,1)S(1)}, bf16[32,24,128]{2,1,0:T(8,128)(2,1)S(1)}, u32[]{:S(2)}, u32[]{:S(2)}) collective-permute-start(bf16[32,24,128]{2,1,0:T(8,128)(2,1)S(1)} %copy-done.1), channel_id=1, source_target_pairs={{0,1},{1,2},{2,3},{3,0},{4,5},{5,6},{6,7},{7,4},{8,9},{9,10},{10,1... | collective-permute-start | bytes 589832 | tf_op jit(solution)/shard_map/ppermute | solution.py:492
  29.4 16.8 %collective-permute-start.3 = (bf16[32,24,128]{2,1,0:T(8,128)(2,1)S(1)}, bf16[32,24,128]{2,1,0:T(8,128)(2,1)S(1)}, u32[]{:S(2)}, u32[]{:S(2)}) collective-permute-start(bf16[32,24,128]{2,1,0:T(8,128)(2,1)S(1)} %collective-permute-done.refs_2_), channel_id=1, source_target_pairs={{0,3},{1,0},{2,1},{3,2},{4,7},{5,4},{6,5},{7,6},{8,11},{9,8},{10,9... | collective-permute-start | bytes 589832 | tf_op jit(solution)/shard_map/ppermute | solution.py:492
  29.9 16.3 %collective-permute-start.2 = (bf16[32,24,128]{2,1,0:T(8,128)(2,1)S(1)}, bf16[32,24,128]{2,1,0:T(8,128)(2,1)S(1)}, u32[]{:S(2)}, u32[]{:S(2)}) collective-permute-start(bf16[32,24,128]{2,1,0:T(8,128)(2,1)S(1)} %collective-permute-done.refs_2_), channel_id=1, source_target_pairs={{0,2},{1,3},{2,0},{3,1},{4,6},{5,7},{6,4},{7,5},{8,10},{9,11},{10,... | collective-permute-start | bytes 589832 | tf_op jit(solution)/shard_map/ppermute | solution.py:492
  35.6 10.7 %collective-permute-start.1 = (bf16[32,24,128]{2,1,0:T(8,128)(2,1)S(1)}, bf16[32,24,128]{2,1,0:T(8,128)(2,1)S(1)}, u32[]{:S(2)}, u32[]{:S(2)}) collective-permute-start(bf16[32,24,128]{2,1,0:T(8,128)(2,1)S(1)} %collective-permute-done.refs_2_), channel_id=1, source_target_pairs={{0,1},{1,2},{2,3},{3,0},{4,5},{5,6},{6,7},{7,4},{8,9},{9,10},{10,1... | collective-permute-start | bytes 589832 | tf_op jit(solution)/shard_map/ppermute | solution.py:492
  46.2 48.8 %copy-start = (f32[16,4096]{1,0:T(8,128)S(1)}, f32[16,4096]{1,0:T(8,128)}, u32[]{:S(2)}) copy-start(f32[16,4096]{1,0:T(8,128)} %refs_9_.3) | copy-start | bytes 786436
  46.2 48.8 %copy-start.2 = (s32[4096]{0:T(1024)S(1)}, s32[4096]{0:T(1024)}, u32[]{:S(2)}) copy-start(s32[4096]{0:T(1024)} %param.12) | copy-start | bytes 49156
  46.3 48.8 %copy-start.3 = (s32[32,128]{1,0:T(8,128)S(1)}, s32[32,128]{1,0:T(8,128)}, u32[]{:S(2)}) copy-start(s32[32,128]{1,0:T(8,128)} %get-tuple-element.54.refs_10_) | copy-start | bytes 49156
  46.3 48.7 %copy-start.4 = (f32[6]{0:T(128)S(1)}, f32[6]{0:T(128)}, u32[]{:S(2)}) copy-start(f32[6]{0:T(128)} %type_hard.1) | copy-start | bytes 76
  53.9 22.4 %collective-permute-start.9 = (bf16[32,16,128]{2,1,0:T(8,128)(2,1)S(1)}, bf16[32,16,128]{2,1,0:T(8,128)(2,1)S(1)}, u32[]{:S(2)}, u32[]{:S(2)}) collective-permute-start(bf16[32,16,128]{2,1,0:T(8,128)(2,1)S(1)} %get-tuple-element.41), channel_id=1, source_target_pairs={{0,1},{1,2},{2,3},{3,0},{4,5},{5,6},{6,7},{7,4},{8,9},{9,10},{10,1... | collective-permute-start | bytes 393224 | tf_op jit(solution)/shard_map/ppermute | solution.py:492
  69.1 7.1 %collective-permute-start.10 = (bf16[32,16,128]{2,1,0:T(8,128)(2,1)S(1)}, bf16[32,16,128]{2,1,0:T(8,128)(2,1)S(1)}, u32[]{:S(2)}, u32[]{:S(2)}) collective-permute-start(bf16[32,16,128]{2,1,0:T(8,128)(2,1)S(1)} %get-tuple-element.42), channel_id=1, source_target_pairs={{0,2},{1,3},{2,0},{3,1},{4,6},{5,7},{6,4},{7,5},{8,10},{9,11},{10,... | collective-permute-start | bytes 393224 | tf_op jit(solution)/shard_map/ppermute | solution.py:492
  69.1 7.1 %collective-permute-start.11 = (bf16[32,16,128]{2,1,0:T(8,128)(2,1)S(1)}, bf16[32,16,128]{2,1,0:T(8,128)(2,1)S(1)}, u32[]{:S(2)}, u32[]{:S(2)}) collective-permute-start(bf16[32,16,128]{2,1,0:T(8,128)(2,1)S(1)} %get-tuple-element.43), channel_id=1, source_target_pairs={{0,3},{1,0},{2,1},{3,2},{4,7},{5,4},{6,5},{7,6},{8,11},{9,8},{10,9... | collective-permute-start | bytes 393224 | tf_op jit(solution)/shard_map/ppermute | solution.py:492
  69.8 6.6 %collective-permute-start.13 = (bf16[32,16,128]{2,1,0:T(8,128)(2,1)S(1)}, bf16[32,16,128]{2,1,0:T(8,128)(2,1)S(1)}, u32[]{:S(2)}, u32[]{:S(2)}) collective-permute-start(bf16[32,16,128]{2,1,0:T(8,128)(2,1)S(1)} %get-tuple-element.44), channel_id=1, source_target_pairs={{0,8},{8,16},{16,24},{24,32},{32,40},{40,48},{48,56},{56,64},{64,7... | collective-permute-start | bytes 393224 | tf_op jit(solution)/shard_map/ppermute | solution.py:484
  74.3 9.0 %collective-permute-start.14 = (bf16[32,16,128]{2,1,0:T(8,128)(2,1)S(1)}, bf16[32,16,128]{2,1,0:T(8,128)(2,1)S(1)}, u32[]{:S(2)}, u32[]{:S(2)}) collective-permute-start(bf16[32,16,128]{2,1,0:T(8,128)(2,1)S(1)} %get-tuple-element.45), channel_id=1, source_target_pairs={{0,16},{8,24},{16,32},{24,40},{32,48},{40,56},{48,64},{56,72},{64,... | collective-permute-start | bytes 393224 | tf_op jit(solution)/shard_map/ppermute | solution.py:484
  76.4 13.6 %collective-permute-start.12 = (bf16[32,16,128]{2,1,0:T(8,128)(2,1)S(1)}, bf16[32,16,128]{2,1,0:T(8,128)(2,1)S(1)}, u32[]{:S(2)}, u32[]{:S(2)}) collective-permute-start(bf16[32,16,128]{2,1,0:T(8,128)(2,1)S(1)} %far_sum.1), channel_id=1, source_target_pairs={{0,4},{1,5},{2,6},{3,7},{4,0},{5,1},{6,2},{7,3},{8,12},{9,13},{10,... | collective-permute-start | bytes 393224 | tf_op jit(solution)/shard_map/ppermute | solution.py:488
  83.3 7.5 %collective-permute-start.15 = (bf16[32,16,128]{2,1,0:T(8,128)(2,1)S(1)}, bf16[32,16,128]{2,1,0:T(8,128)(2,1)S(1)}, u32[]{:S(2)}, u32[]{:S(2)}) collective-permute-start(bf16[32,16,128]{2,1,0:T(8,128)(2,1)S(1)} %get-tuple-element.51), channel_id=1, source_target_pairs={{0,1},{1,2},{2,3},{3,0},{4,5},{5,6},{6,7},{7,4},{8,9},{9,10},{10,1... | collective-permute-start | bytes 393224 | tf_op jit(solution)/shard_map/ppermute | solution.py:492
  85.3 7.1 %collective-permute-start.16 = (bf16[32,16,128]{2,1,0:T(8,128)(2,1)S(1)}, bf16[32,16,128]{2,1,0:T(8,128)(2,1)S(1)}, u32[]{:S(2)}, u32[]{:S(2)}) collective-permute-start(bf16[32,16,128]{2,1,0:T(8,128)(2,1)S(1)} %get-tuple-element.52), channel_id=1, source_target_pairs={{0,2},{1,3},{2,0},{3,1},{4,6},{5,7},{6,4},{7,5},{8,10},{9,11},{10,... | collective-permute-start | bytes 393224 | tf_op jit(solution)/shard_map/ppermute | solution.py:492
  90.0 5.0 %collective-permute-start.17 = (bf16[32,16,128]{2,1,0:T(8,128)(2,1)S(1)}, bf16[32,16,128]{2,1,0:T(8,128)(2,1)S(1)}, u32[]{:S(2)}, u32[]{:S(2)}) collective-permute-start(bf16[32,16,128]{2,1,0:T(8,128)(2,1)S(1)} %get-tuple-element.53), channel_id=1, source_target_pairs={{0,3},{1,0},{2,1},{3,2},{4,7},{5,4},{6,5},{7,6},{8,11},{9,8},{10,9... | collective-permute-start | bytes 393224 | tf_op jit(solution)/shard_map/ppermute | solution.py:492
